TPU v7x, 128 devices: a whole 4x4x4 slice. The times are simulated.
128 devices in a mesh: dp: 32 (over z, y, x_lo), tensor: 4 (over x_hi, core).
Axes of the slice: x: 4 (x_hi: 2, x_lo: 2; x = x_hi * 2 + x_lo), y: 4, z: 4, core: 2. Of those that a mesh axis runs over, the one named last changes fastest.
Arguments:
- hidden_in: float32 [4096, 1024], P('dp'), may hold values from -6 to 6
- cotangent: float32 [4096, 1024], P('dp'), may hold values from -6 to 6
- seq_lengths: int32 [32, 4], P('dp'), may hold values from 1 to 64, 128 in all within a row
- routes: int32 [2, 4096, 8], P(None, 'dp'), may hold values from 0 to 31, all different within a row; in each aligned block of 128 rows (0 to 127, 128 to 255, ..., all dimensions but the last counted through in order) at most 48 rows name the same one
- norm_attn: float32 [2, 1024], replicated, may hold values from 0.25 to 1.75
- norm_moe: float32 [2, 1024], replicated, may hold values from 0.25 to 1.75
- w_query: bfloat16 [2, 1024, 1024], P(None, None, 'tensor'), may hold values from -0.1875 to 0.1875
- w_key: bfloat16 [2, 1024, 512], P(None, None, 'tensor'), may hold values from -0.1875 to 0.1875
- w_value: bfloat16 [2, 1024, 512], P(None, None, 'tensor'), may hold values from -0.1875 to 0.1875
- w_output: bfloat16 [2, 1024, 1024], P(None, 'tensor'), may hold values from -0.75 to 0.75
- w_router: bfloat16 [2, 1024, 32], replicated, may hold values from -0.375 to 0.375
- w_gate: bfloat16 [2, 32, 1024, 512], P(None, 'dp', None, 'tensor'), may hold values from -0.1875 to 0.1875
- w_up: bfloat16 [2, 32, 1024, 512], P(None, 'dp', None, 'tensor'), may hold values from -0.1875 to 0.1875
- w_down: bfloat16 [2, 32, 512, 1024], P(None, 'dp', 'tensor'), may hold values from -0.375 to 0.375
Outputs:
- output: float32 [4096, 1024], P('dp')
- d_hidden_in: float32 [4096, 1024], P('dp')
- d_norm_attn: float32 [2, 1024], P(None, 'dp')
- d_norm_moe: float32 [2, 1024], P(None, 'dp')
- d_w_query: float32 [2, 1024, 1024], P(None, 'dp', 'tensor')
- d_w_key: float32 [2, 1024, 512], P(None, 'dp', 'tensor')
- d_w_value: float32 [2, 1024, 512], P(None, 'dp', 'tensor')
- d_w_output: float32 [2, 1024, 1024], P(None, 'tensor', 'dp')
- d_w_router: float32 [2, 1024, 32], P(None, 'dp')
- d_w_gate: float32 [2, 32, 1024, 512], P(None, 'dp', None, 'tensor')
- d_w_up: float32 [2, 32, 1024, 512], P(None, 'dp', None, 'tensor')
- d_w_down: float32 [2, 32, 512, 1024], P(None, 'dp', 'tensor')
Inputs may be any that keep to these rules, and one draw needn't show every extreme that they name: `seq_lengths`: each row sums to 128 and its largest entry is 64. `routes`: each token names 8 different experts in each layer; among the 128 tokens of one index of dp no expert is named more than 48 times in a layer, a bound that some block reaches there.
All inputs are finite; a program needn't handle non-finite values.
Results may differ from a plain program's by a relative error of at most 0.03.
Values may be sent and summed in bfloat16 or wider, within the bound.
No kernel may reach another device: no remote copies, remote signals or barrier semaphores. Data moves between devices by JAX's collectives and lax.ppermute only.
A program may use at most 128 MiB of HBM per device.

v0:
```python
import jax
import jax.numpy as jnp
from jax import lax
from jax.sharding import PartitionSpec as P

HD = 64
E = 32
CAP = 48


EPS = 1e-05
SCALE = 0.125
NEGATIVE = -1e30


def norm_forward(hidden, gain):
    inverse_root = lax.rsqrt(jnp.mean(hidden * hidden, axis=-1, keepdims=True) + EPS)
    return (hidden * inverse_root * gain, inverse_root)


def norm_backward(hidden, inverse_root, gain, d_normed):
    scaled = gain * d_normed
    d_hidden = inverse_root * (
        scaled
        - hidden * inverse_root * inverse_root * jnp.mean(scaled * hidden, axis=-1, keepdims=True)
    )
    d_gain = jnp.sum(d_normed * hidden * inverse_root, axis=0)
    return (d_hidden, d_gain)


def rope_tables(lengths, count):
    ends = jnp.cumsum(lengths)
    starts = ends - lengths
    index = jnp.arange(count, dtype=jnp.int32)
    segment = jnp.sum((index[:, None] >= ends[None, :]).astype(jnp.int32), axis=1)
    member = segment[:, None] == jnp.arange(lengths.shape[0], dtype=jnp.int32)[None, :]
    begin = jnp.sum(jnp.where(member, starts[None, :], 0), axis=1)
    position = (index - begin).astype(jnp.float32)
    half = HD // 2
    inverse = jnp.exp(-jnp.log(10000.0) * jnp.arange(half, dtype=jnp.float32) * 2.0 / HD)
    angle = position[:, None] * inverse[None, :]
    allowed = (segment[:, None] == segment[None, :]) & (index[None, :] <= index[:, None])
    return (jnp.cos(angle), jnp.sin(angle), allowed)


def rotate(values, cosine, sine):
    half = values.shape[-1] // 2
    first, second = (values[..., :half], values[..., half:])
    cos_rows, sin_rows = (cosine[:, None, :], sine[:, None, :])
    return jnp.concatenate(
        [first * cos_rows - second * sin_rows, second * cos_rows + first * sin_rows], axis=-1
    )


def unrotate(values, cosine, sine):
    half = values.shape[-1] // 2
    first, second = (values[..., :half], values[..., half:])
    cos_rows, sin_rows = (cosine[:, None, :], sine[:, None, :])
    return jnp.concatenate(
        [first * cos_rows + second * sin_rows, second * cos_rows - first * sin_rows], axis=-1
    )


def slots_for(routing):
    count, top = routing.shape
    onehot = (routing[:, :, None] == jnp.arange(E, dtype=jnp.int32)[None, None, :]).astype(
        jnp.int32
    )
    per_token = jnp.sum(onehot, axis=1)
    before = jnp.cumsum(per_token, axis=0) - per_token
    rank = jnp.sum(onehot * before[:, None, :], axis=2)
    slot = routing * CAP + rank
    pair = (
        jnp.full((E * CAP,), count * top, jnp.int32)
        .at[slot.reshape(-1)]
        .set(jnp.arange(count * top, dtype=jnp.int32))
    )
    token = pair // top
    return (onehot, slot, pair, token)


def project_heads(normed_b, weight, cosine, sine, turn):
    raw = jnp.dot(normed_b, weight, preferred_element_type=jnp.float32)
    shaped = raw.reshape(raw.shape[0], -1, HD)
    if turn:
        shaped = rotate(shaped, cosine, sine)
    return shaped.astype(jnp.bfloat16)


def attend(query, keys, values, allowed):
    count, kv_heads, size = keys.shape
    group = query.shape[1] // kv_heads
    grouped = query.reshape(count, kv_heads, group, size)
    scores = jnp.einsum("qkgd,tkd->kgqt", grouped, keys, preferred_element_type=jnp.float32) * SCALE
    scores = jnp.where(allowed[None, None], scores, NEGATIVE)
    top = jnp.max(scores, axis=-1, keepdims=True)
    expd = jnp.exp(scores - top)
    total = jnp.sum(expd, axis=-1, keepdims=True)
    lse = top + jnp.log(total)
    probs = (expd / total).astype(jnp.bfloat16)
    mixed = jnp.einsum("kgqt,tkd->qkgd", probs, values, preferred_element_type=jnp.float32)
    return (mixed.reshape(count, -1).astype(jnp.bfloat16), lse)


def attend_back(query, keys, values, lse, allowed, d_mixed):
    count, kv_heads, size = keys.shape
    group = query.shape[1] // kv_heads
    grouped = query.reshape(count, kv_heads, group, size)
    scores = jnp.einsum("qkgd,tkd->kgqt", grouped, keys, preferred_element_type=jnp.float32) * SCALE
    probs = jnp.where(allowed[None, None], jnp.exp(scores - lse), 0.0)
    probs_b = probs.astype(jnp.bfloat16)
    d_grouped = d_mixed.reshape(count, kv_heads, group, size)
    d_values = jnp.einsum("kgqt,qkgd->tkd", probs_b, d_grouped, preferred_element_type=jnp.float32)
    d_probs = jnp.einsum("qkgd,tkd->kgqt", d_grouped, values, preferred_element_type=jnp.float32)
    delta = jnp.sum(probs * d_probs, axis=-1, keepdims=True)
    d_scores = (probs * (d_probs - delta) * SCALE).astype(jnp.bfloat16)
    d_query = jnp.einsum(
        "kgqt,tkd->qkgd", d_scores, keys, preferred_element_type=jnp.float32
    ).reshape(count, -1, size)
    d_keys = jnp.einsum("kgqt,qkgd->tkd", d_scores, grouped, preferred_element_type=jnp.float32)
    return (d_query, d_keys, d_values)


def head_total(partial_value):
    return lax.psum(partial_value, "tensor")


def to_owners(rows):
    arrived = lax.all_to_all(rows, "dp", split_axis=0, concat_axis=0, tiled=True)
    return arrived


def from_owners(partial_value):
    summed = lax.psum_scatter(
        partial_value.astype(jnp.bfloat16), "tensor", scatter_dimension=1, tiled=True
    )
    full = lax.all_gather(summed, "tensor", axis=1, tiled=True)
    back = lax.all_to_all(full, "dp", split_axis=0, concat_axis=0, tiled=True)
    return back


def expert_weights_for(gate_w, up_w, down_w):
    full = (gate_w, up_w, down_w)
    slots_each = CAP
    return (full, slots_each)


def expert_forward(received, gate_w, up_w, down_w, slots_each):
    blocks = received.reshape(-1, gate_w.shape[0], slots_each, received.shape[1])
    gate = jnp.einsum("sxcd,xdf->sxcf", blocks, gate_w, preferred_element_type=jnp.float32)
    upper = jnp.einsum("sxcd,xdf->sxcf", blocks, up_w, preferred_element_type=jnp.float32)
    act = (gate * jax.nn.sigmoid(gate) * upper).astype(jnp.bfloat16)
    partial_value = jnp.einsum("sxcf,xfd->sxcd", act, down_w, preferred_element_type=jnp.float32)
    return partial_value.reshape(received.shape[0], -1)


def expert_backward(received, d_received, gate_w, up_w, down_w, slots_each):
    blocks = received.reshape(-1, gate_w.shape[0], slots_each, received.shape[1])
    d_blocks = d_received.reshape(blocks.shape)
    gate = jnp.einsum("sxcd,xdf->sxcf", blocks, gate_w, preferred_element_type=jnp.float32)
    upper = jnp.einsum("sxcd,xdf->sxcf", blocks, up_w, preferred_element_type=jnp.float32)
    sig = jax.nn.sigmoid(gate)
    act = (gate * sig * upper).astype(jnp.bfloat16)
    d_act = jnp.einsum("sxcd,xfd->sxcf", d_blocks, down_w, preferred_element_type=jnp.float32)
    d_down = jnp.einsum("sxcf,sxcd->xfd", act, d_blocks, preferred_element_type=jnp.float32)
    d_upper = (d_act * gate * sig).astype(jnp.bfloat16)
    d_gate = (d_act * upper * sig * (1.0 + gate * (1.0 - sig))).astype(jnp.bfloat16)
    d_gate_w = jnp.einsum("sxcd,sxcf->xdf", blocks, d_gate, preferred_element_type=jnp.float32)
    d_up_w = jnp.einsum("sxcd,sxcf->xdf", blocks, d_upper, preferred_element_type=jnp.float32)
    d_inputs = jnp.einsum(
        "sxcf,xdf->sxcd", d_gate, gate_w, preferred_element_type=jnp.float32
    ) + jnp.einsum("sxcf,xdf->sxcd", d_upper, up_w, preferred_element_type=jnp.float32)
    return (d_inputs.reshape(received.shape[0], -1), d_gate_w, d_up_w, d_down)


def per_device(
    hidden_in,
    cotangent,
    seq_lengths,
    routes,
    norm_attn,
    norm_moe,
    w_query,
    w_key,
    w_value,
    w_output,
    w_router,
    w_gate,
    w_up,
    w_down,
):
    count = hidden_in.shape[0]
    layers = w_query.shape[0]
    cosine, sine, allowed = rope_tables(seq_lengths[0], count)
    hidden = hidden_in
    kept = []
    for layer in range(layers):
        normed, inverse_one = norm_forward(hidden, norm_attn[layer])
        normed_b = normed.astype(jnp.bfloat16)
        query = project_heads(normed_b, w_query[layer], cosine, sine, True)
        keys = project_heads(normed_b, w_key[layer], cosine, sine, True)
        values = project_heads(normed_b, w_value[layer], cosine, sine, False)
        mixed, lse = attend(query, keys, values, allowed)
        attn_part = jnp.dot(mixed, w_output[layer], preferred_element_type=jnp.float32)
        middle = hidden + head_total(attn_part)
        normed_two, inverse_two = norm_forward(middle, norm_moe[layer])
        moe_in = normed_two.astype(jnp.bfloat16)
        logits = jnp.dot(moe_in, w_router[layer], preferred_element_type=jnp.float32)
        onehot, slot, pair, token = slots_for(routes[layer])
        chosen = jnp.sum(jnp.where(onehot > 0, logits[:, None, :], 0.0), axis=2)
        gates = jax.nn.softmax(chosen, axis=-1)
        padded = jnp.concatenate([moe_in, jnp.zeros((1, moe_in.shape[1]), jnp.bfloat16)], axis=0)
        expert_set, slots_each = expert_weights_for(w_gate[layer], w_up[layer], w_down[layer])
        received = to_owners(padded[token])
        partial_value = expert_forward(
            received, expert_set[0], expert_set[1], expert_set[2], slots_each
        )
        returned = from_owners(partial_value)
        picked = returned[slot]
        kept.append(
            (
                hidden,
                normed_b,
                inverse_one,
                query,
                keys,
                values,
                mixed,
                lse,
                middle,
                moe_in,
                inverse_two,
                gates,
                onehot,
                slot,
                pair,
                received,
                picked,
                expert_set,
                slots_each,
            )
        )
        hidden = middle + jnp.sum(gates[:, :, None] * picked, axis=1)
    d_hidden = cotangent
    layer_sums = [None] * layers
    expert_grads = [None] * layers
    for layer in reversed(range(layers)):
        (
            layer_input,
            normed_b,
            inverse_one,
            query,
            keys,
            values,
            mixed,
            lse,
            middle,
            moe_in,
            inverse_two,
            gates,
            onehot,
            slot,
            pair,
            received,
            picked,
            expert_set,
            slots_each,
        ) = kept[layer]
        d_gates = jnp.sum(picked * d_hidden[:, None, :], axis=-1)
        d_chosen = gates * (d_gates - jnp.sum(gates * d_gates, axis=-1, keepdims=True))
        d_logits = jnp.sum(onehot.astype(jnp.float32) * d_chosen[:, :, None], axis=1)
        d_picked = (gates[:, :, None] * d_hidden[:, None, :]).astype(jnp.bfloat16)
        flat = d_picked.reshape(-1, d_picked.shape[2])
        padded = jnp.concatenate([flat, jnp.zeros((1, flat.shape[1]), jnp.bfloat16)], axis=0)
        d_received = to_owners(padded[pair])
        d_part, d_gate_w, d_up_w, d_down_w = expert_backward(
            received, d_received, expert_set[0], expert_set[1], expert_set[2], slots_each
        )
        d_rows = from_owners(d_part)
        router_f = w_router[layer].astype(jnp.float32)
        d_normed_two = jnp.sum(d_rows[slot], axis=1, dtype=jnp.float32) + jnp.dot(
            d_logits, router_f.T, precision=lax.Precision.HIGHEST
        )
        d_router = jnp.dot(moe_in.astype(jnp.float32).T, d_logits, precision=lax.Precision.HIGHEST)
        d_mid_norm, d_gain_two = norm_backward(middle, inverse_two, norm_moe[layer], d_normed_two)
        d_middle = d_hidden + d_mid_norm
        d_middle_b = d_middle.astype(jnp.bfloat16)
        d_output_w = jnp.dot(mixed.T, d_middle_b, preferred_element_type=jnp.float32)
        d_mixed = jnp.dot(d_middle_b, w_output[layer].T, preferred_element_type=jnp.float32).astype(
            jnp.bfloat16
        )
        d_query, d_keys, d_values = attend_back(query, keys, values, lse, allowed, d_mixed)
        d_query = unrotate(d_query, cosine, sine).reshape(count, -1).astype(jnp.bfloat16)
        d_keys = unrotate(d_keys, cosine, sine).reshape(count, -1).astype(jnp.bfloat16)
        d_values = d_values.reshape(count, -1).astype(jnp.bfloat16)
        d_query_w = jnp.dot(normed_b.T, d_query, preferred_element_type=jnp.float32)
        d_key_w = jnp.dot(normed_b.T, d_keys, preferred_element_type=jnp.float32)
        d_value_w = jnp.dot(normed_b.T, d_values, preferred_element_type=jnp.float32)
        d_normed_part = (
            jnp.dot(d_query, w_query[layer].T, preferred_element_type=jnp.float32)
            + jnp.dot(d_keys, w_key[layer].T, preferred_element_type=jnp.float32)
            + jnp.dot(d_values, w_value[layer].T, preferred_element_type=jnp.float32)
        )
        d_normed_one = head_total(d_normed_part)
        d_hid_norm, d_gain_one = norm_backward(
            layer_input, inverse_one, norm_attn[layer], d_normed_one
        )
        d_hidden = d_middle + d_hid_norm
        local = (d_query_w, d_key_w, d_value_w, d_output_w, d_gain_one, d_gain_two, d_router)
        layer_sums[layer] = local
        expert_grads[layer] = (d_gate_w, d_up_w, d_down_w)
    stacked = tuple(
        (jnp.stack([layer_sums[layer][item] for layer in range(layers)]) for item in range(7))
    )
    stacked = (
        lax.psum_scatter(
            stacked[0].astype(jnp.bfloat16), "dp", scatter_dimension=1, tiled=True
        ).astype(jnp.float32),
        lax.psum_scatter(
            stacked[1].astype(jnp.bfloat16), "dp", scatter_dimension=1, tiled=True
        ).astype(jnp.float32),
        lax.psum_scatter(
            stacked[2].astype(jnp.bfloat16), "dp", scatter_dimension=1, tiled=True
        ).astype(jnp.float32),
        lax.psum_scatter(
            stacked[3].astype(jnp.bfloat16), "dp", scatter_dimension=2, tiled=True
        ).astype(jnp.float32),
        lax.psum_scatter(
            stacked[4].astype(jnp.bfloat16), "dp", scatter_dimension=1, tiled=True
        ).astype(jnp.float32),
        lax.psum_scatter(
            stacked[5].astype(jnp.bfloat16), "dp", scatter_dimension=1, tiled=True
        ).astype(jnp.float32),
        lax.psum_scatter(
            stacked[6].astype(jnp.bfloat16), "dp", scatter_dimension=1, tiled=True
        ).astype(jnp.float32),
    )
    expert_stack = [
        jnp.stack([expert_grads[layer][item] for layer in range(layers)]) for item in range(3)
    ]
    return (
        hidden,
        d_hidden,
        stacked[4],
        stacked[5],
        stacked[0],
        stacked[1],
        stacked[2],
        stacked[3],
        stacked[6],
        expert_stack[0],
        expert_stack[1],
        expert_stack[2],
    )


def solution(mesh):
    in_specs = (
        P("dp", None),
        P("dp", None),
        P("dp", None),
        P(None, "dp", None),
        P(),
        P(),
        P(None, None, "tensor"),
        P(None, None, "tensor"),
        P(None, None, "tensor"),
        P(None, "tensor", None),
        P(),
        P(None, "dp", None, "tensor"),
        P(None, "dp", None, "tensor"),
        P(None, "dp", "tensor", None),
    )
    out_specs = (
        P("dp", None),
        P("dp", None),
        P(None, "dp"),
        P(None, "dp"),
        P(None, "dp", "tensor"),
        P(None, "dp", "tensor"),
        P(None, "dp", "tensor"),
        P(None, "tensor", "dp"),
        P(None, "dp", None),
        P(None, "dp", None, "tensor"),
        P(None, "dp", None, "tensor"),
        P(None, "dp", "tensor", None),
    )
    return jax.shard_map(
        per_device, mesh=mesh, in_specs=in_specs, out_specs=out_specs, check_vma=False
    )
```

profile of v0, /device:TPU:0, one launch (start us, length us, event | category | flops | bytes accessed | tf_op | source)
XLA Modules:
  0.0 2268.3 jit_solution(6154448703244310012)
XLA Ops:
  22.7 4.3 scatter_custom_fusion
  27.6 38.0 %all-reduce.11.cloned.1.call-done = f32[128,1024]{1,0:T(8,128)} async-done(((f32[128,1024]{1,0:T(8,128)}), f32[128,1024]{1,0:T(8,128)}) %all-reduce.11.cloned.1.call-update) | async-done | bytes 524304 | tf_op jit(solution)/shard_map/psum | solution.py:125
  68.5 5.8 gather_fusion
  74.3 48.3 %all_to_all.84 = bf16[32,48,1024]{2,1,0:T(8,128)(2,1)S(1)} all-to-all(bf16[32,48,1024]{2,1,0:T(8,128)(2,1)} %bitcast.490), channel_id=1, replica_groups=mesh['dp'=32,'tensor'=4] {'dp'}, dimensions={0} | all-to-all | bytes 6291456 | tf_op jit(solution)/shard_map/all_to_all | solution.py:129
  126.7 2.6 convolution_convert_fusion.1
  129.4 41.2 %reduce-scatter.17.cloned.1.call-done = bf16[1536,256]{1,0:T(8,128)(2,1)} async-done(((bf16[1536,1024]{1,0:T(8,128)(2,1)}), bf16[1536,256]{1,0:T(8,128)(2,1)}) %reduce-scatter.17.cloned.1.call-update) | async-done | bytes 786448 | tf_op jit(solution)/shard_map/reduce_scatter | solution.py:134
  170.6 34.0 %all-gather.5.cloned.1.call-done = bf16[1536,1024]{1,0:T(8,128)(2,1)} async-done(((bf16[1536,256]{1,0:T(8,128)(2,1)}), bf16[1536,1024]{1,0:T(8,128)(2,1)}) %all-gather.5.cloned.1.call-update) | async-done | bytes 3145744 | tf_op jit(solution)/shard_map/all_gather | solution.py:137
  204.7 7.4 all-to-all-start.1
  223.1 2.0 copy.155
  227.6 28.2 %all-to-all-done.1 = bf16[32,48,1024]{2,1,0:T(8,128)(2,1)S(1)} async-done(((bf16[32,48,1024]{2,1,0:T(8,128)(2,1)}), bf16[32,48,1024]{2,1,0:T(8,128)(2,1)S(1)}, u32[]{:S(2)}, u32[]{:S(2)}) %all-to-all-start.1) | async-done | bytes 3145760 | tf_op jit(solution)/shard_map/all_to_all | solution.py:138
  255.8 5.4 gather_fusion.1
  261.2 3.0 fusion.4
  268.9 4.3 scatter_custom_fusion.1
  273.2 37.9 %all-reduce.13.cloned.1.call-done = f32[128,1024]{1,0:T(8,128)} async-done(((f32[128,1024]{1,0:T(8,128)}), f32[128,1024]{1,0:T(8,128)}) %all-reduce.13.cloned.1.call-update) | async-done | bytes 524304 | tf_op jit(solution)/shard_map/psum | solution.py:125
  313.3 5.8 gather_fusion.2
  319.2 7.5 all-to-all-start.2
  328.3 5.9 gather_fusion.4
  334.1 36.9 %all-to-all-done.2 = bf16[32,48,1024]{2,1,0:T(8,128)(2,1)} async-done(((bf16[32,48,1024]{2,1,0:T(8,128)(2,1)}), bf16[32,48,1024]{2,1,0:T(8,128)(2,1)}, u32[]{:S(2)}, u32[]{:S(2)}) %all-to-all-start.2) | async-done | bytes 3145760 | tf_op jit(solution)/shard_map/all_to_all | solution.py:129
  371.0 7.7 all-to-all-start.4
  379.0 3.8 convolution_bitcast_fusion.2
  382.8 3.8 convolution_bitcast_fusion.3
  386.6 34.4 %all-to-all-done.4 = bf16[32,48,1024]{2,1,0:T(8,128)(2,1)S(1)} async-done(((bf16[32,48,1024]{2,1,0:T(8,128)(2,1)}), bf16[32,48,1024]{2,1,0:T(8,128)(2,1)S(1)}, u32[]{:S(2)}, u32[]{:S(2)}) %all-to-all-start.4) | async-done | bytes 3145760 | tf_op jit(solution)/shard_map/all_to_all | solution.py:129
  421.0 4.7 multiply_convert_fusion.2
  426.4 2.6 convolution_convert_fusion
  430.3 2.7 add_convert_fusion.1
  433.1 38.9 %reduce-scatter.19.cloned.1.call-done = bf16[1536,256]{1,0:T(8,128)(2,1)} async-done(((bf16[1536,1024]{1,0:T(8,128)(2,1)}), bf16[1536,256]{1,0:T(8,128)(2,1)}) %reduce-scatter.19.cloned.1.call-update) | async-done | bytes 786448 | tf_op jit(solution)/shard_map/reduce_scatter | solution.py:134
  472.0 46.5 %reduce-scatter.21.cloned.1.call-done = bf16[1536,256]{1,0:T(8,128)(2,1)} async-done(((bf16[1536,1024]{1,0:T(8,128)(2,1)}), bf16[1536,256]{1,0:T(8,128)(2,1)}) %reduce-scatter.21.cloned.1.call-update) | async-done | bytes 786448 | tf_op jit(solution)/shard_map/reduce_scatter | solution.py:134
  518.5 34.0 %all-gather.7.cloned.1.call-done = bf16[1536,1024]{1,0:T(8,128)(2,1)} async-done(((bf16[1536,256]{1,0:T(8,128)(2,1)}), bf16[1536,1024]{1,0:T(8,128)(2,1)}) %all-gather.7.cloned.1.call-update) | async-done | bytes 3145744 | tf_op jit(solution)/shard_map/all_gather | solution.py:137
  552.6 7.3 all-to-all-start.3
  559.9 43.8 %all-gather.9.cloned.1.call-done = bf16[1536,1024]{1,0:T(8,128)(2,1)} async-done(((bf16[1536,256]{1,0:T(8,128)(2,1)}), bf16[1536,1024]{1,0:T(8,128)(2,1)}) %all-gather.9.cloned.1.call-update) | async-done | bytes 3145744 | tf_op jit(solution)/shard_map/all_gather | solution.py:137
  603.7 13.8 all-to-all-done.3
  619.1 4.1 all-to-all-start.5
  626.0 8.3 gather_fusion.3
  634.4 4.2 fusion.3
  640.2 24.5 %all-to-all-done.5 = bf16[32,48,1024]{2,1,0:T(8,128)(2,1)S(1)} async-done(((bf16[32,48,1024]{2,1,0:T(8,128)(2,1)}), bf16[32,48,1024]{2,1,0:T(8,128)(2,1)S(1)}, u32[]{:S(2)}, u32[]{:S(2)}) %all-to-all-start.5) | async-done | bytes 3145760 | tf_op jit(solution)/shard_map/all_to_all | solution.py:138
  664.7 5.4 gather_fusion.5
  670.1 3.1 convert_reduce_fusion.1
  673.3 2.3 multiply_reduce_fusion
  686.2 38.0 %all-reduce.15.cloned.1.call-done = f32[128,1024]{1,0:T(8,128)} async-done(((f32[128,1024]{1,0:T(8,128)}), f32[128,1024]{1,0:T(8,128)}) %all-reduce.15.cloned.1.call-update) | async-done | bytes 524304 | tf_op jit(solution)/shard_map/psum | solution.py:125
  728.5 5.9 gather_fusion.6
  734.4 48.3 %all_to_all.85 = bf16[32,48,1024]{2,1,0:T(8,128)(2,1)S(1)} all-to-all(bf16[32,48,1024]{2,1,0:T(8,128)(2,1)} %bitcast.491), channel_id=1, replica_groups=mesh['dp'=32,'tensor'=4] {'dp'}, dimensions={0} | all-to-all | bytes 6291456 | tf_op jit(solution)/shard_map/all_to_all | solution.py:129
  785.7 2.6 add_convert_fusion
  788.4 41.2 %reduce-scatter.23.cloned.1.call-done = bf16[1536,256]{1,0:T(8,128)(2,1)} async-done(((bf16[1536,1024]{1,0:T(8,128)(2,1)}), bf16[1536,256]{1,0:T(8,128)(2,1)}) %reduce-scatter.23.cloned.1.call-update) | async-done | bytes 786448 | tf_op jit(solution)/shard_map/reduce_scatter | solution.py:134
  829.6 34.1 %all-gather.11.cloned.1.call-done = bf16[1536,1024]{1,0:T(8,128)(2,1)} async-done(((bf16[1536,256]{1,0:T(8,128)(2,1)}), bf16[1536,1024]{1,0:T(8,128)(2,1)}) %all-gather.11.cloned.1.call-update) | async-done | bytes 3145744 | tf_op jit(solution)/shard_map/all_gather | solution.py:137
  863.7 7.6 all-to-all-start.7
  872.6 2.8 fusion.5
  878.3 36.7 %all-to-all-done.7 = bf16[32,48,1024]{2,1,0:T(8,128)(2,1)S(1)} async-done(((bf16[32,48,1024]{2,1,0:T(8,128)(2,1)}), bf16[32,48,1024]{2,1,0:T(8,128)(2,1)S(1)}, u32[]{:S(2)}, u32[]{:S(2)}) %all-to-all-start.7) | async-done | bytes 3145760 | tf_op jit(solution)/shard_map/all_to_all | solution.py:138
  915.0 5.4 gather_fusion.7
  920.3 3.2 convert_reduce_fusion
  927.8 2.2 convolution_bitcast_fusion.15
  930.0 2.2 fusion.33
  943.2 35.5 %all-reduce.17.cloned.1.call-done = f32[128,1024]{1,0:T(8,128)} async-done(((f32[128,1024]{1,0:T(8,128)}), f32[128,1024]{1,0:T(8,128)}) %all-reduce.17.cloned.1.call-update) | async-done | bytes 524304 | tf_op jit(solution)/shard_map/psum | solution.py:125
  982.1 2.1 copy.178
  987.0 3.7 convolution_bitcast_fusion.8
  992.4 2.5 convolution_bitcast_fusion.6
  994.9 3.7 convolution_bitcast_fusion.10
  999.0 143.3 %reduce-scatter.35.cloned.1.call-done = bf16[32,64]{1,0:T(8,128)(2,1)} async-done(((bf16[1024,64]{1,0:T(8,128)(2,1)}), bf16[32,64]{1,0:T(8,128)(2,1)}) %reduce-scatter.35.cloned.1.call-update) | async-done | bytes 4112
  1145.3 2.6 convolution_bitcast_fusion.7
  1153.2 149.1 %reduce-scatter.33.cloned.1.call-done = bf16[32,2]{1,0:T(8,128)(2,1)} async-done(((bf16[1024,2]{1,0:T(8,128)(2,1)}), bf16[32,2]{1,0:T(8,128)(2,1)}) %reduce-scatter.33.cloned.1.call-update) | async-done | bytes 144
  1304.7 157.7 %reduce-scatter.31.cloned.1.call-done = bf16[32,2]{1,0:T(8,128)(2,1)} async-done(((bf16[1024,2]{1,0:T(8,128)(2,1)}), bf16[32,2]{1,0:T(8,128)(2,1)}) %reduce-scatter.31.cloned.1.call-update) | async-done | bytes 144
  1463.7 308.9 %all-reduce.19.cloned.1.call-done = bf16[2,256,1024]{1,0,2:T(2,128)(2,1)} async-done(((bf16[2,256,1024]{1,0,2:T(2,128)(2,1)}), bf16[2,256,1024]{1,0,2:T(2,128)(2,1)}) %all-reduce.19.cloned.1.call-update) | async-done | bytes 1048592
  1774.0 163.1 %reduce-scatter.27.cloned.1.call-done = bf16[2,32,128]{2,1,0:T(8,128)(2,1)} async-done(((bf16[2,1024,128]{2,1,0:T(8,128)(2,1)}), bf16[2,32,128]{2,1,0:T(8,128)(2,1)}) %reduce-scatter.27.cloned.1.call-update) | async-done | bytes 16400 | tf_op jit(solution)/shard_map/reduce_scatter | solution.py:319
  1938.5 159.6 %reduce-scatter.29.cloned.1.call-done = bf16[2,32,128]{2,1,0:T(8,128)(2,1)} async-done(((bf16[2,1024,128]{2,1,0:T(8,128)(2,1)}), bf16[2,32,128]{2,1,0:T(8,128)(2,1)}) %reduce-scatter.29.cloned.1.call-update) | async-done | bytes 16400 | tf_op jit(solution)/shard_map/reduce_scatter | solution.py:322
  2099.3 160.8 %reduce-scatter.25.cloned.1.call-done = bf16[2,32,256]{2,1,0:T(8,128)(2,1)} async-done(((bf16[2,1024,256]{2,1,0:T(8,128)(2,1)}), bf16[2,32,256]{2,1,0:T(8,128)(2,1)}) %reduce-scatter.25.cloned.1.call-update) | async-done | bytes 32784 | tf_op jit(solution)/shard_map/reduce_scatter | solution.py:316
  (496 shorter events, 114.5 us)
Async XLA Ops:
  7.2 9.0 copy-start.25
  7.2 58.4 %all-reduce.11.cloned.1.call-start = ((), (), s32[]{:S(2)}) async-start(), calls=%async_computation.18 | async-start | bytes 1048576 | tf_op jit(solution)/shard_map/psum | solution.py:125
  11.1 254.4 %copy-start.85 = (f32[1,1024]{1,0:T(1,128)}, f32[1,1024]{1,0:T(1,128)S(1)}, u32[]{:S(2)}) copy-start(f32[1,1024]{1,0:T(1,128)S(1)} %get-tuple-element.129) | copy-start | bytes 12292
  17.3 10.3 copy-start.120
  17.7 49.0 %copy-start.99 = (bf16[128,2,32]{0,2,1:T(8,128)(2,1)}, bf16[128,2,32]{0,2,1:T(8,128)(2,1)S(1)}, u32[]{:S(2)}) copy-start(bf16[128,2,32]{0,2,1:T(8,128)(2,1)S(1)} %get-tuple-element.115) | copy-start | bytes 49156
  17.8 49.0 %copy-start.100 = (bf16[128,2,32]{0,2,1:T(8,128)(2,1)}, bf16[128,2,32]{0,2,1:T(8,128)(2,1)S(1)}, u32[]{:S(2)}) copy-start(bf16[128,2,32]{0,2,1:T(8,128)(2,1)S(1)} %get-tuple-element.116) | copy-start | bytes 49156
  18.1 49.7 %copy-start.48 = (f32[2,2,128,128]{2,3,1,0:T(8,128)}, f32[2,2,128,128]{2,3,1,0:T(8,128)S(1)}, u32[]{:S(2)}) copy-start(f32[2,2,128,128]{2,3,1,0:T(8,128)S(1)} %get-tuple-element.134) | copy-start | bytes 786436
  18.1 49.7 %copy-start.106 = (f32[2,2,128]{2,1,0:T(2,128)}, f32[2,2,128]{2,1,0:T(2,128)S(1)}, u32[]{:S(2)}) copy-start(f32[2,2,128]{2,1,0:T(2,128)S(1)} %get-tuple-element.133) | copy-start | bytes 6148
  18.5 50.0 %copy-start.108 = (f32[2,2,128]{2,1,0:T(2,128)}, f32[2,2,128]{2,1,0:T(2,128)S(1)}, u32[]{:S(2)}) copy-start(f32[2,2,128]{2,1,0:T(2,128)S(1)} %fusion.114) | copy-start | bytes 6148
  19.5 54.8 %copy-start.77 = (bf16[2,64,2,128]{3,1,2,0:T(8,128)(2,1)}, bf16[2,64,2,128]{3,1,2,0:T(8,128)(2,1)S(1)}, u32[]{:S(2)}) copy-start(bf16[2,64,2,128]{3,1,2,0:T(8,128)(2,1)S(1)} %convolution_convert_fusion.15) | copy-start | bytes 196612
  20.6 150.0 %reduce-scatter.17.cloned.1.call-start = ((), (), s32[]{:S(2)}) async-start(), calls=%async_computation.19 | async-start | bytes 3932160 | tf_op jit(solution)/shard_map/reduce_scatter | solution.py:134
  21.2 305.7 %copy-start.82 = (s32[128,8]{0,1:T(8,128)}, s32[128,8]{0,1:T(8,128)S(1)}, u32[]{:S(2)}) copy-start(s32[128,8]{0,1:T(8,128)S(1)} %get-tuple-element.123) | copy-start | bytes 12292
  27.6 46.7 %copy-start.87 = (f32[1,1024]{1,0:T(1,128)}, f32[1,1024]{1,0:T(1,128)S(1)}, u32[]{:S(2)}) copy-start(f32[1,1024]{1,0:T(1,128)S(1)} %get-tuple-element.128) | copy-start | bytes 12292
  27.6 284.7 %copy-start.89 = (f32[1,1024]{1,0:T(1,128)}, f32[1,1024]{1,0:T(1,128)S(1)}, u32[]{:S(2)}) copy-start(f32[1,1024]{1,0:T(1,128)S(1)} %get-tuple-element.127) | copy-start | bytes 12292
  74.3 48.3 %copy-start.37 = (bf16[2,1,1024,128]{3,2,1,0:T(8,128)(2,1)S(1)}, bf16[2,1,1024,128]{3,2,1,0:T(8,128)(2,1)}, u32[]{:S(2)}) copy-start(bf16[2,1,1024,128]{3,2,1,0:T(8,128)(2,1)} %param.25) | copy-start | bytes 1572868
  129.3 75.3 %all-gather.5.cloned.1.call-start = ((), (), s32[]{:S(2)}) async-start(), calls=%async_computation.20 | async-start | bytes 3932160 | tf_op jit(solution)/shard_map/all_gather | solution.py:137
  204.7 12.5 copy-start.96
  204.7 51.1 %all-to-all-start.1 = ((bf16[32,48,1024]{2,1,0:T(8,128)(2,1)}), bf16[32,48,1024]{2,1,0:T(8,128)(2,1)S(1)}, u32[]{:S(2)}, u32[]{:S(2)}) async-start(bf16[32,48,1024]{2,1,0:T(8,128)(2,1)} %bitcast.492), calls=%async_computation.2 | async-start | bytes 6291456 | tf_op jit(solution)/shard_map/all_to_all | solution.py:138
  212.1 99.0 %all-reduce.13.cloned.1.call-start = ((), (), s32[]{:S(2)}) async-start(), calls=%async_computation.21 | async-start | bytes 1048576 | tf_op jit(solution)/shard_map/psum | solution.py:125
  227.5 33.6 %copy-start.58 = (f32[128,8]{1,0:T(8,128)}, f32[128,8]{1,0:T(8,128)S(1)}, u32[]{:S(2)}) copy-start(f32[128,8]{1,0:T(8,128)S(1)} %copy.146) | copy-start | bytes 12292
  265.5 45.7 %copy-start.3 = (f32[128,1024]{1,0:T(8,128)}, f32[128,1024]{1,0:T(8,128)S(1)}, u32[]{:S(2)}) copy-start(f32[128,1024]{1,0:T(8,128)S(1)} %get-tuple-element.85) | copy-start | bytes 1572868
  266.2 46.1 %copy-start.7 = (bf16[128,1024]{1,0:T(8,128)(2,1)}, bf16[128,1024]{1,0:T(8,128)(2,1)S(1)}, u32[]{:S(2)}) copy-start(bf16[128,1024]{1,0:T(8,128)(2,1)S(1)} %multiply_convert_fusion.7) | copy-start | bytes 786436
  266.8 46.4 %copy-start.80 = (bf16[128,2,64,1]{0,2,3,1:T(8,128)(2,1)}, bf16[128,2,64,1]{0,2,3,1:T(8,128)(2,1)S(1)}, u32[]{:S(2)}) copy-start(bf16[128,2,64,1]{0,2,3,1:T(8,128)(2,1)S(1)} %fusion.31) | copy-start | bytes 98308
  267.1 46.2 %copy-start.93 = (bf16[128,4,32]{0,2,1:T(8,128)(2,1)}, bf16[128,4,32]{0,2,1:T(8,128)(2,1)S(1)}, u32[]{:S(2)}) copy-start(bf16[128,4,32]{0,2,1:T(8,128)(2,1)S(1)} %get-tuple-element.105) | copy-start | bytes 98308
  267.1 46.2 %copy-start.94 = (bf16[128,4,32]{0,2,1:T(8,128)(2,1)}, bf16[128,4,32]{0,2,1:T(8,128)(2,1)S(1)}, u32[]{:S(2)}) copy-start(bf16[128,4,32]{0,2,1:T(8,128)(2,1)S(1)} %get-tuple-element.106) | copy-start | bytes 98308
  267.2 46.1 %copy-start.102 = (bf16[128,2,32]{0,2,1:T(8,128)(2,1)}, bf16[128,2,32]{0,2,1:T(8,128)(2,1)S(1)}, u32[]{:S(2)}) copy-start(bf16[128,2,32]{0,2,1:T(8,128)(2,1)S(1)} %get-tuple-element.114) | copy-start | bytes 49156
  267.4 51.7 %copy-start.50 = (f32[2,2,128,128]{2,3,1,0:T(8,128)}, f32[2,2,128,128]{2,3,1,0:T(8,128)S(1)}, u32[]{:S(2)}) copy-start(f32[2,2,128,128]{2,3,1,0:T(8,128)S(1)} %get-tuple-element.138) | copy-start | bytes 786436
  267.5 51.6 %copy-start.113 = (f32[2,2,128]{2,1,0:T(2,128)}, f32[2,2,128]{2,1,0:T(2,128)S(1)}, u32[]{:S(2)}) copy-start(f32[2,2,128]{2,1,0:T(2,128)S(1)} %fusion.115) | copy-start | bytes 6148
  267.7 51.4 %copy-start.78 = (bf16[2,64,2,128]{3,1,2,0:T(8,128)(2,1)}, bf16[2,64,2,128]{3,1,2,0:T(8,128)(2,1)S(1)}, u32[]{:S(2)}) copy-start(bf16[2,64,2,128]{3,1,2,0:T(8,128)(2,1)S(1)} %convolution_convert_fusion.14) | copy-start | bytes 196612
  313.2 13.5 copy-start.30
  319.2 51.8 %all-to-all-start.2 = ((bf16[32,48,1024]{2,1,0:T(8,128)(2,1)}), bf16[32,48,1024]{2,1,0:T(8,128)(2,1)}, u32[]{:S(2)}, u32[]{:S(2)}) async-start(bf16[32,48,1024]{2,1,0:T(8,128)(2,1)} %bitcast.488), calls=%async_computation.3 | async-start | bytes 6291456 | tf_op jit(solution)/shard_map/all_to_all | solution.py:129
  371.0 49.9 %all-to-all-start.4 = ((bf16[32,48,1024]{2,1,0:T(8,128)(2,1)}), bf16[32,48,1024]{2,1,0:T(8,128)(2,1)S(1)}, u32[]{:S(2)}, u32[]{:S(2)}) async-start(bf16[32,48,1024]{2,1,0:T(8,128)(2,1)} %bitcast.489), calls=%async_computation.6 | async-start | bytes 6291456 | tf_op jit(solution)/shard_map/all_to_all | solution.py:129
  378.7 93.2 %reduce-scatter.19.cloned.1.call-start = ((), (), s32[]{:S(2)}) async-start(), calls=%async_computation.22 | async-start | bytes 3932160 | tf_op jit(solution)/shard_map/reduce_scatter | solution.py:134
  429.1 89.5 %reduce-scatter.21.cloned.1.call-start = ((), (), s32[]{:S(2)}) async-start(), calls=%async_computation.24 | async-start | bytes 3932160 | tf_op jit(solution)/shard_map/reduce_scatter | solution.py:134
  433.0 119.6 %all-gather.7.cloned.1.call-start = ((), (), s32[]{:S(2)}) async-start(), calls=%async_computation.23 | async-start | bytes 3932160 | tf_op jit(solution)/shard_map/all_gather | solution.py:137
  472.0 131.7 %all-gather.9.cloned.1.call-start = ((), (), s32[]{:S(2)}) async-start(), calls=%async_computation.25 | async-start | bytes 3932160 | tf_op jit(solution)/shard_map/all_gather | solution.py:137
  552.6 64.9 %all-to-all-start.3 = ((bf16[32,48,1024]{2,1,0:T(8,128)(2,1)}), bf16[32,48,1024]{2,1,0:T(8,128)(2,1)S(1)}, u32[]{:S(2)}, u32[]{:S(2)}) async-start(bf16[32,48,1024]{2,1,0:T(8,128)(2,1)} %bitcast.495), calls=%async_computation.5 | async-start | bytes 6291456 | tf_op jit(solution)/shard_map/all_to_all | solution.py:138
  619.1 45.6 %all-to-all-start.5 = ((bf16[32,48,1024]{2,1,0:T(8,128)(2,1)}), bf16[32,48,1024]{2,1,0:T(8,128)(2,1)S(1)}, u32[]{:S(2)}, u32[]{:S(2)}) async-start(bf16[32,48,1024]{2,1,0:T(8,128)(2,1)} %bitcast.493), calls=%async_computation.8 | async-start | bytes 6291456 | tf_op jit(solution)/shard_map/all_to_all | solution.py:138
  623.2 101.0 %all-reduce.15.cloned.1.call-start = ((), (), s32[]{:S(2)}) async-start(), calls=%async_computation.26 | async-start | bytes 1048576 | tf_op jit(solution)/shard_map/psum | solution.py:125
  676.6 49.4 %copy-start.15 = (f32[128,1024]{1,0:T(8,128)}, f32[128,1024]{1,0:T(8,128)S(1)}, u32[]{:S(2)}) copy-start(f32[128,1024]{1,0:T(8,128)S(1)} %get-tuple-element.95) | copy-start | bytes 1572868
  678.1 46.1 %copy-start.4 = (f32[128,1024]{1,0:T(8,128)S(1)}, f32[128,1024]{1,0:T(8,128)}, u32[]{:S(2)}) copy-start(f32[128,1024]{1,0:T(8,128)} %copy-done.3) | copy-start | bytes 1572868
  678.1 46.1 %copy-start.86 = (f32[1,1024]{1,0:T(1,128)S(1)}, f32[1,1024]{1,0:T(1,128)}, u32[]{:S(2)}) copy-start(f32[1,1024]{1,0:T(1,128)} %copy-done.85) | copy-start | bytes 12292
  681.3 45.9 %copy-start.75 = (bf16[128,2,64]{0,2,1:T(8,128)(2,1)}, bf16[128,2,64]{0,2,1:T(8,128)(2,1)S(1)}, u32[]{:S(2)}) copy-start(bf16[128,2,64]{0,2,1:T(8,128)(2,1)S(1)} %maximum_convert_fusion.2) | copy-start | bytes 98308
  684.5 145.0 %reduce-scatter.23.cloned.1.call-start = ((), (), s32[]{:S(2)}) async-start(), calls=%async_computation.27 | async-start | bytes 3932160 | tf_op jit(solution)/shard_map/reduce_scatter | solution.py:134
  734.4 48.3 %copy-start.55 = (f32[32,1,48,128]{3,2,0,1:T(8,128)S(1)}, f32[32,1,48,128]{3,2,0,1:T(8,128)}, u32[]{:S(2)}) copy-start(f32[32,1,48,128]{3,2,0,1:T(8,128)} %copy-done.54) | copy-start | bytes 2359300
  734.4 48.3 %copy-start.64 = (bf16[2,1,128,1024]{3,2,1,0:T(8,128)(2,1)S(1)}, bf16[2,1,128,1024]{3,2,1,0:T(8,128)(2,1)}, u32[]{:S(2)}) copy-start(bf16[2,1,128,1024]{3,2,1,0:T(8,128)(2,1)} %param.27) | copy-start | bytes 1572868
  734.4 48.3 %copy-start.129 = (f32[32,1,48,128]{3,2,0,1:T(8,128)S(1)}, f32[32,1,48,128]{3,2,0,1:T(8,128)}, u32[]{:S(2)}) copy-start(f32[32,1,48,128]{3,2,0,1:T(8,128)} %get-tuple-element.136) | copy-start | bytes 2359300
  788.3 75.3 %all-gather.11.cloned.1.call-start = ((), (), s32[]{:S(2)}) async-start(), calls=%async_computation.28 | async-start | bytes 3932160 | tf_op jit(solution)/shard_map/all_gather | solution.py:137
  863.7 51.3 %all-to-all-start.7 = ((bf16[32,48,1024]{2,1,0:T(8,128)(2,1)}), bf16[32,48,1024]{2,1,0:T(8,128)(2,1)S(1)}, u32[]{:S(2)}, u32[]{:S(2)}) async-start(bf16[32,48,1024]{2,1,0:T(8,128)(2,1)} %bitcast.494), calls=%async_computation.11 | async-start | bytes 6291456 | tf_op jit(solution)/shard_map/all_to_all | solution.py:138
  871.3 107.4 %all-reduce.17.cloned.1.call-start = ((), (), s32[]{:S(2)}) async-start(), calls=%async_computation.29 | async-start | bytes 1048576 | tf_op jit(solution)/shard_map/psum | solution.py:125
  925.6 8.9 copy-start.36
  936.3 42.3 %copy-start.2 = (f32[128,1024]{1,0:T(8,128)S(1)}, f32[128,1024]{1,0:T(8,128)}, u32[]{:S(2)}) copy-start(f32[128,1024]{1,0:T(8,128)} %param.14) | copy-start | bytes 1572868
  936.3 42.3 %copy-start.84 = (f32[1,1024]{1,0:T(1,128)S(1)}, f32[1,1024]{1,0:T(1,128)}, u32[]{:S(2)}) copy-start(f32[1,1024]{1,0:T(1,128)} %copy-done.83) | copy-start | bytes 12292
  936.3 42.3 %copy-start.124 = (f32[128]{0:T(128)S(1)}, f32[128]{0:T(128)}, u32[]{:S(2)}) copy-start(f32[128]{0:T(128)} %copy-done.123) | copy-start | bytes 1540
  936.4 205.9 %reduce-scatter.35.cloned.1.call-start = ((), (), s32[]{:S(2)}) async-start(), calls=%async_computation.35 | async-start | bytes 270336
  939.0 363.3 %reduce-scatter.33.cloned.1.call-start = ((), (), s32[]{:S(2)}) async-start(), calls=%async_computation.34 | async-start | bytes 270336
  943.1 519.2 %reduce-scatter.31.cloned.1.call-start = ((), (), s32[]{:S(2)}) async-start(), calls=%async_computation.33 | async-start | bytes 270336
  980.8 791.7 %all-reduce.19.cloned.1.call-start = ((), (), s32[]{:S(2)}) async-start(), calls=%async_computation.36 | async-start | bytes 2097152
  984.1 953.0 %reduce-scatter.27.cloned.1.call-start = ((), (), s32[]{:S(2)}) async-start(), calls=%async_computation.31 | async-start | bytes 540672 | tf_op jit(solution)/shard_map/reduce_scatter | solution.py:319
  985.6 1112.4 %reduce-scatter.29.cloned.1.call-start = ((), (), s32[]{:S(2)}) async-start(), calls=%async_computation.32 | async-start | bytes 540672 | tf_op jit(solution)/shard_map/reduce_scatter | solution.py:322
  992.2 1268.0 %reduce-scatter.25.cloned.1.call-start = ((), (), s32[]{:S(2)}) async-start(), calls=%async_computation.30 | async-start | bytes 1081344 | tf_op jit(solution)/shard_map/reduce_scatter | solution.py:316
  994.9 149.0 %copy-start.57 = (bf16[128,4,64]{0,2,1:T(8,128)(2,1)S(1)}, bf16[128,4,64]{0,2,1:T(8,128)(2,1)}, u32[]{:S(2)}) copy-start(bf16[128,4,64]{0,2,1:T(8,128)(2,1)} %copy-done.56) | copy-start | bytes 196612
  998.7 146.6 %copy-start.42 = (bf16[32,1,48,128]{3,2,0,1:T(8,128)(2,1)S(1)}, bf16[32,1,48,128]{3,2,0,1:T(8,128)(2,1)}, u32[]{:S(2)}) copy-start(bf16[32,1,48,128]{3,2,0,1:T(8,128)(2,1)} %copy-done.41) | copy-start | bytes 1179652
  1151.1 152.5 %copy-start.33 = (f32[128,1024]{1,0:T(8,128)S(1)}, f32[128,1024]{1,0:T(8,128)}, u32[]{:S(2)}) copy-start(f32[128,1024]{1,0:T(8,128)} %all-reduce.17.cloned.1.call-done) | copy-start | bytes 1572868
  (91 other events, 365.0 us)
Sparse Core Ops, SparseCore 0:
  20.7 44.8 all-reduce.10
  129.4 41.1 reduce-scatter.16
  172.3 32.3 all-gather.4
  268.9 42.1 all-reduce.12
  429.2 42.7 reduce-scatter.18
  474.4 44.0 reduce-scatter.20
  520.2 32.3 all-gather.6
  554.2 49.4 all-gather.8
  684.7 39.4 all-reduce.14
  788.5 41.0 reduce-scatter.22
  831.3 32.3 all-gather.10
  936.5 42.1 all-reduce.16
  981.0 161.2 reduce-scatter.34
  1144.5 157.7 reduce-scatter.32
  1304.5 157.7 reduce-scatter.30
  1464.6 307.8 all-reduce.18
  1774.8 162.3 reduce-scatter.26
  1939.3 158.6 reduce-scatter.28
  2100.4 159.7 reduce-scatter.24
where the time goes:
time: 2280 us; the launch traced here: 2270 us
  waiting for transfers between devices  1880 us (82%)
  local copies, waits for them, and re-layouts  98 us (4%)
  blocking collectives  96.5 us (4%)
  matrix products  77 us (3%)
  other arithmetic  56.2 us (2%)
  starting transfers between devices  43.4 us (2%)
    unnamed x23, waiting for transfers between devices  759 us
    reduce_scatter x4, waiting for transfers between devices, from_owners(): lax.psum_scatter(partial_value.astype(jnp.bfloat16), 'tensor', scatter_di...  168 us
    reduce_scatter x1, waiting for transfers between devices, per_device(): lax.psum_scatter(stacked[1].astype(jnp.bfloat16), 'dp', scatter_dimension...  163 us
    reduce_scatter x1, waiting for transfers between devices, per_device(): lax.psum_scatter(stacked[0].astype(jnp.bfloat16), 'dp', scatter_dimension...  161 us
    reduce_scatter x1, waiting for transfers between devices, per_device(): lax.psum_scatter(stacked[2].astype(jnp.bfloat16), 'dp', scatter_dimension...  160 us
    psum x4, waiting for transfers between devices, head_total(): return lax.psum(partial_value, 'tensor')  149 us
    all_gather x4, waiting for transfers between devices, from_owners(): full = lax.all_gather(summed, 'tensor', axis=1, tiled=True)  146 us
    all_to_all x4, waiting for transfers between devices, from_owners(): back = lax.all_to_all(full, 'dp', split_axis=0, concat_axis=0, tiled=True)  103 us
  transfers between devices with their start and end apart: 25, of which 25 were waited for; matrix products, arithmetic and copies ran while one was open for 5% of the time, Pallas kernels for 0%

commit v1 on v0

v1 whole, which is shorter than its diff:
```python
import functools
import jax
import jax.numpy as jnp
from jax import lax
from jax.experimental import pallas as pl
from jax.experimental.pallas import tpu as pltpu
from jax.sharding import PartitionSpec as P

HD = 64
E = 32
WAYS = 4
ROOM = 16
EPS = 1e-05
SCALE = 0.125
NEGATIVE = -1e30
F32 = jnp.float32
BF16 = jnp.bfloat16


def dot(a, b, ca=1, cb=0, precision=None):
    return lax.dot_general(
        a, b, (((ca,), (cb,)), ((), ())), preferred_element_type=F32, precision=precision
    )


def norm_forward(hidden, gain):
    inverse_root = lax.rsqrt(jnp.mean(hidden * hidden, axis=-1, keepdims=True) + EPS)
    return (hidden * inverse_root * gain, inverse_root)


def norm_backward(hidden, inverse_root, gain, d_normed):
    scaled = gain * d_normed
    d_hidden = inverse_root * (
        scaled
        - hidden * inverse_root * inverse_root * jnp.mean(scaled * hidden, axis=-1, keepdims=True)
    )
    d_gain = jnp.sum(d_normed * hidden * inverse_root, axis=0)
    return (d_hidden, d_gain)


def rope_tables(lengths, count):
    ends = jnp.cumsum(lengths)
    starts = ends - lengths
    index = jnp.arange(count, dtype=jnp.int32)
    segment = jnp.sum((index[:, None] >= ends[None, :]).astype(jnp.int32), axis=1)
    member = segment[:, None] == jnp.arange(lengths.shape[0], dtype=jnp.int32)[None, :]
    begin = jnp.sum(jnp.where(member, starts[None, :], 0), axis=1)
    position = (index - begin).astype(F32)
    half = HD // 2
    inverse = jnp.exp(-jnp.log(10000.0) * jnp.arange(half, dtype=F32) * 2.0 / HD)
    angle = position[:, None] * inverse[None, :]
    allowed = (segment[:, None] == segment[None, :]) & (index[None, :] <= index[:, None])
    return (jnp.cos(angle), jnp.sin(angle), allowed)


def rotate(values, cosine, sine):
    half = values.shape[-1] // 2
    first, second = (values[..., :half], values[..., half:])
    cos_rows, sin_rows = (cosine[:, None, :], sine[:, None, :])
    return jnp.concatenate(
        [first * cos_rows - second * sin_rows, second * cos_rows + first * sin_rows], axis=-1
    )


def unrotate(values, cosine, sine):
    return rotate(values, cosine, -sine)


def project_heads(normed_b, weight, cosine, sine, turn):
    raw = dot(normed_b, weight)
    shaped = raw.reshape(raw.shape[0], -1, HD)
    if turn:
        shaped = rotate(shaped, cosine, sine)
    return shaped.astype(BF16)


def attend(query, keys, values, allowed):
    count, kv_heads, size = keys.shape
    group = query.shape[1] // kv_heads
    grouped = query.reshape(count, kv_heads, group, size)
    scores = jnp.einsum("qkgd,tkd->kgqt", grouped, keys, preferred_element_type=F32) * SCALE
    scores = jnp.where(allowed[None, None], scores, NEGATIVE)
    top = jnp.max(scores, axis=-1, keepdims=True)
    expd = jnp.exp(scores - top)
    total = jnp.sum(expd, axis=-1, keepdims=True)
    lse = top + jnp.log(total)
    probs = (expd / total).astype(BF16)
    mixed = jnp.einsum("kgqt,tkd->qkgd", probs, values, preferred_element_type=F32)
    return (mixed.reshape(count, -1).astype(BF16), lse)


def attend_back(query, keys, values, lse, allowed, d_mixed):
    count, kv_heads, size = keys.shape
    group = query.shape[1] // kv_heads
    grouped = query.reshape(count, kv_heads, group, size)
    scores = jnp.einsum("qkgd,tkd->kgqt", grouped, keys, preferred_element_type=F32) * SCALE
    probs = jnp.where(allowed[None, None], jnp.exp(scores - lse), 0.0)
    probs_b = probs.astype(BF16)
    d_grouped = d_mixed.reshape(count, kv_heads, group, size)
    d_values = jnp.einsum("kgqt,qkgd->tkd", probs_b, d_grouped, preferred_element_type=F32)
    d_probs = jnp.einsum("qkgd,tkd->kgqt", d_grouped, values, preferred_element_type=F32)
    delta = jnp.sum(probs * d_probs, axis=-1, keepdims=True)
    d_scores = (probs * (d_probs - delta) * SCALE).astype(BF16)
    d_query = jnp.einsum("kgqt,tkd->qkgd", d_scores, keys, preferred_element_type=F32)
    d_keys = jnp.einsum("kgqt,qkgd->tkd", d_scores, grouped, preferred_element_type=F32)
    return (d_query.reshape(count, -1, size), d_keys, d_values)


def swap(value, mask):
    return lax.ppermute(value, "tensor", [(i, i ^ mask) for i in range(WAYS)])


def tensor_total(part):
    mine = lax.optimization_barrier(part.astype(BF16))
    pair = lax.optimization_barrier((mine.astype(F32) + swap(mine, 1).astype(F32)).astype(BF16))
    return pair.astype(F32) + swap(pair, 2).astype(F32)


def exchange(rows):
    return lax.all_to_all(rows, "dp", split_axis=0, concat_axis=0, tiled=True)


def dp_total(part):
    arrived = exchange(part.astype(BF16))
    return jnp.sum(arrived.reshape(E, -1, part.shape[1]).astype(F32), axis=0)


def expert_kernel(want_out, want_back, *refs):
    refs = list(refs)
    rows = refs.pop(0)[...]
    d_rows = refs.pop(0)[...] if want_back else None
    pairs, downs, refs = refs[:WAYS], refs[WAYS : 2 * WAYS], refs[2 * WAYS :]
    out_ref = refs.pop(0) if want_out else None
    if want_back:
        d_rows_ref = refs.pop(0)
        d_pairs, d_downs, refs = refs[:WAYS], refs[WAYS : 2 * WAYS], refs[2 * WAYS :]
    out_sum = refs.pop(0) if want_out else None
    back_sum = refs.pop(0) if want_back else None
    for block in range(WAYS):
        both = dot(rows, pairs[block][...])
        width = both.shape[1] // 2
        gate, upper = both[:, :width], both[:, width:]
        sig = jax.nn.sigmoid(gate)
        act = (gate * sig * upper).astype(BF16)
        if want_out:
            term = dot(act, downs[block][...])
            out_sum[...] = term if block == 0 else out_sum[...] + term
        if want_back:
            d_act = dot(d_rows, downs[block][...], 1, 1)
            d_downs[block][...] = dot(act, d_rows, 0, 0).astype(d_downs[block].dtype)
            d_upper = (d_act * gate * sig).astype(BF16)
            d_gate = (d_act * upper * sig * (1.0 + gate * (1.0 - sig))).astype(BF16)
            d_both = jnp.concatenate([d_gate, d_upper], axis=1)
            term = dot(d_both, pairs[block][...], 1, 1)
            back_sum[...] = term if block == 0 else back_sum[...] + term
            d_pairs[block][...] = dot(rows, d_both, 0, 0).astype(d_pairs[block].dtype)
    if want_out:
        out_ref[...] = out_sum[...].astype(BF16)
    if want_back:
        d_rows_ref[...] = back_sum[...].astype(BF16)


def experts(rows, d_rows, weights, want_out):
    pairs, downs = weights
    want_back = d_rows is not None
    args = [rows] + ([d_rows] if want_back else []) + list(pairs) + list(downs)
    like = jax.ShapeDtypeStruct(rows.shape, BF16)
    outs = [like] if want_out else []
    kinds = (F32, BF16, F32, BF16)
    if want_back:
        outs = outs + [like]
        outs = outs + [jax.ShapeDtypeStruct(w.shape, k) for w, k in zip(pairs, kinds)]
        outs = outs + [jax.ShapeDtypeStruct(w.shape, k) for w, k in zip(downs, kinds)]
    sums = [pltpu.VMEM(rows.shape, F32)] * (int(want_out) + int(want_back))
    vmem = pl.BlockSpec(memory_space=pltpu.VMEM)
    products = 2 * rows.shape[0] * rows.shape[1] * 128 * WAYS
    return pl.pallas_call(
        functools.partial(expert_kernel, want_out, want_back),
        out_shape=tuple(outs),
        in_specs=[vmem] * len(args),
        out_specs=tuple([vmem] * len(outs)),
        scratch_shapes=sums,
        cost_estimate=pl.CostEstimate(
            flops=products * (3 + 6 * int(want_back)), bytes_accessed=8 << 20, transcendentals=0
        ),
        name="experts_back" if want_back else "experts",
    )(*args)


def spread_out(own):
    far = swap(own, 2)
    return (own, swap(own, 1), far, swap(far, 1))


def gather_weights(gate_w, up_w, down_w):
    own_pair = jnp.concatenate([gate_w, up_w], axis=1)
    return (spread_out(own_pair), spread_out(down_w))


def reduce_blocks(blocks):
    near = blocks[0] + swap(blocks[1], 1).astype(F32)
    far = blocks[2] + swap(blocks[3], 1).astype(F32)
    return near + swap(far.astype(BF16), 2).astype(F32)


def slot_tables(routing, me):
    count = routing.shape[0]
    member = jnp.any(routing[:, :, None] == jnp.arange(E, dtype=jnp.int32)[None, None, :], axis=1)
    index = jnp.arange(count, dtype=jnp.int32)
    before = (index[:, None] > index[None, :]).astype(BF16)
    rank = dot(before, member.astype(BF16))
    code = jnp.where(member, rank, -1.0).astype(BF16)
    slots = jnp.arange(E * ROOM, dtype=jnp.int32)
    widen = (slots[None, :] // ROOM == jnp.arange(E, dtype=jnp.int32)[:, None]).astype(BF16)
    wanted = (slots % ROOM) * WAYS + me
    pick = dot(code, widen) == wanted[None, :].astype(F32)
    return (member, pick, widen)


def attention_forward(hidden, gain, weights, rope):
    wq, wk, wv, wo = weights
    cosine, sine, allowed = rope
    normed, inverse = norm_forward(hidden, gain)
    normed_b = normed.astype(BF16)
    query = project_heads(normed_b, wq, cosine, sine, True)
    keys = project_heads(normed_b, wk, cosine, sine, True)
    values = project_heads(normed_b, wv, cosine, sine, False)
    mixed, lse = attend(query, keys, values, allowed)
    part = dot(mixed, wo)
    return part, (normed_b, inverse, query, keys, values, mixed, lse)


def attention_backward(d_middle_b, saved, weights, rope):
    wq, wk, wv, wo = weights
    cosine, sine, allowed = rope
    normed_b, inverse, query, keys, values, mixed, lse = saved
    count = normed_b.shape[0]
    d_mixed = dot(d_middle_b, wo, 1, 1).astype(BF16)
    d_query, d_keys, d_values = attend_back(query, keys, values, lse, allowed, d_mixed)
    d_query = unrotate(d_query, cosine, sine).reshape(count, -1).astype(BF16)
    d_keys = unrotate(d_keys, cosine, sine).reshape(count, -1).astype(BF16)
    d_values = d_values.reshape(count, -1).astype(BF16)
    part = dot(d_query, wq, 1, 1) + dot(d_keys, wk, 1, 1) + dot(d_values, wv, 1, 1)
    d_all = jnp.concatenate([d_query, d_keys, d_values], axis=1)
    return part, d_all


def router(middle, gain, w_router, tables):
    member, pick, widen = tables
    normed, inverse = norm_forward(middle, gain)
    moe_in = normed.astype(BF16)
    logits = jnp.where(member, dot(moe_in, w_router), NEGATIVE)
    top = jnp.max(logits, axis=-1, keepdims=True)
    expd = jnp.where(member, jnp.exp(logits - top), 0.0)
    gates = expd / jnp.sum(expd, axis=-1, keepdims=True)
    shares = jnp.where(pick, dot(gates.astype(BF16), widen), 0.0).astype(BF16)
    return moe_in, inverse, gates, shares


def gate_gradient(d_hidden_b, picked, gates, shares, widen):
    q = dot(
        dot(d_hidden_b, picked, 1, 1) * shares.astype(F32),
        widen.astype(F32),
        1,
        1,
        lax.Precision.HIGHEST,
    )
    return q - gates * jnp.sum(q, axis=-1, keepdims=True)


def columns(*parts):
    rows = parts[0].shape[0]
    width = sum(p.shape[1] for p in parts)
    pad = -width % 128
    parts = [p.astype(BF16) for p in parts]
    if pad:
        parts.append(jnp.zeros((rows, pad), BF16))
    return jnp.concatenate(parts, axis=1)


def per_device(
    hidden_in,
    cotangent,
    seq_lengths,
    routes,
    norm_attn,
    norm_moe,
    w_query,
    w_key,
    w_value,
    w_output,
    w_router,
    w_gate,
    w_up,
    w_down,
):
    count, width = hidden_in.shape
    me = lax.axis_index("tensor")
    rope = rope_tables(seq_lengths[0], count)
    expert_weights = [gather_weights(w_gate[l, 0], w_up[l, 0], w_down[l, 0]) for l in range(2)]
    tables = [slot_tables(routes[l], me) for l in range(2)]
    attn_weights = [(w_query[l], w_key[l], w_value[l], w_output[l]) for l in range(2)]
    slots = E * ROOM

    def middle_of(hidden, layer):
        part, saved = attention_forward(hidden, norm_attn[layer], attn_weights[layer], rope)
        return hidden + tensor_total(part), saved

    def moe_backward(layer, middle, inverse, moe_in, gates, d_log_part, back, d_hidden):
        pick = tables[layer][1].astype(BF16)
        payload = jnp.concatenate(
            [dot(pick, back), d_log_part, jnp.zeros((count, 128 - E), F32)], axis=1
        )
        summed = tensor_total(payload)
        d_logits = summed[:, width : width + E]
        router_f = w_router[layer].astype(F32)
        d_normed = summed[:, :width] + dot(d_logits, router_f, 1, 1, lax.Precision.HIGHEST)
        d_router = dot(moe_in, d_logits.astype(BF16), 0, 0)
        d_norm, d_gain = norm_backward(middle, inverse, norm_moe[layer], d_normed)
        return d_hidden + d_norm, d_gain, d_router

    def attn_backward(layer, hidden, saved, d_middle):
        d_middle_b = d_middle.astype(BF16)
        d_output_t = dot(d_middle_b, saved[5], 0, 0)
        part, d_all = attention_backward(d_middle_b, saved, attn_weights[layer], rope)
        d_in_w = dot(saved[0], d_all, 0, 0)
        d_norm, d_gain = norm_backward(
            hidden, saved[1], norm_attn[layer], tensor_total(part)
        )
        return d_middle + d_norm, d_gain, d_in_w, d_output_t

    middle0, saved0 = middle_of(hidden_in, 0)
    moe_in0, inverse0, gates0, shares0 = router(middle0, norm_moe[0], w_router[0], tables[0])
    send = dot(tables[0][1].astype(BF16), moe_in0, 0, 0).astype(BF16)
    received0 = exchange(send)
    (out,) = experts(received0, None, expert_weights[0], True)
    picked0 = exchange(out)
    hidden1 = middle0 + tensor_total(dot(shares0, picked0))

    middle1, saved1 = middle_of(hidden1, 1)
    moe_in1, inverse1, gates1, shares1 = router(middle1, norm_moe[1], w_router[1], tables[1])
    cot_b = cotangent.astype(BF16)
    send = dot(tables[1][1].astype(BF16), moe_in1, 0, 0).astype(BF16)
    d_send = dot(shares1, cot_b, 0, 0).astype(BF16)

    def couple(a, b):
        a, b = a.reshape(E, ROOM, width), b.reshape(E, ROOM, width)
        both = exchange(jnp.concatenate([a, b], axis=1).reshape(2 * slots, width))
        both = both.reshape(E, 2 * ROOM, width)
        return both[:, :ROOM].reshape(slots, width), both[:, ROOM:].reshape(slots, width)

    received1, d_received1 = couple(send, d_send)
    out, d_in, *expert_grads1 = experts(received1, d_received1, expert_weights[1], True)
    picked1, back1 = couple(out, d_in)
    d_log_part = gate_gradient(cot_b, picked1, gates1, shares1, tables[1][2])
    d_middle1, d_gain_two1, d_router1 = moe_backward(
        1, middle1, inverse1, moe_in1, gates1, d_log_part, back1, cotangent
    )
    output = middle1 + tensor_total(dot(shares1, picked1))
    d_hidden1, d_gain_one1, d_in_w1, d_output_t1 = attn_backward(1, hidden1, saved1, d_middle1)

    d_hidden1_b = d_hidden1.astype(BF16)
    d_send = dot(shares0, d_hidden1_b, 0, 0).astype(BF16)
    d_received0 = exchange(d_send)
    d_in, *expert_grads0 = experts(received0, d_received0, expert_weights[0], False)
    back0 = exchange(d_in)
    d_log_part = gate_gradient(d_hidden1_b, picked0, gates0, shares0, tables[0][2])
    d_middle0, d_gain_two0, d_router0 = moe_backward(
        0, middle0, inverse0, moe_in0, gates0, d_log_part, back0, d_hidden1
    )
    d_hidden0, d_gain_one0, d_in_w0, d_output_t0 = attn_backward(0, hidden_in, saved0, d_middle0)

    sums1 = dp_total(
        columns(d_in_w1, d_output_t1, d_router1, d_gain_one1[:, None], d_gain_two1[:, None])
    )
    early0 = dp_total(columns(d_output_t0, d_router0, d_gain_two0[:, None]))
    late0 = dp_total(columns(d_in_w0, d_gain_one0[:, None]))
    sums0 = jnp.concatenate(
        [late0[:, :512], early0[:, :288], late0[:, 512:513], early0[:, 288:289]], axis=1
    )
    both = jnp.stack([sums0, sums1[:, :802]])
    pair_grads = jnp.stack([reduce_blocks(g[:WAYS]) for g in (expert_grads0, expert_grads1)])
    down_grads = jnp.stack([reduce_blocks(g[WAYS:]) for g in (expert_grads0, expert_grads1)])
    return (
        output,
        d_hidden0,
        both[:, :, 800],
        both[:, :, 801],
        both[:, :, :256],
        both[:, :, 256:384],
        both[:, :, 384:512],
        jnp.swapaxes(both[:, :, 512:768], 1, 2),
        both[:, :, 768:800],
        pair_grads[:, None, :, :128],
        pair_grads[:, None, :, 128:],
        down_grads[:, None],
    )


def solution(mesh):
    in_specs = (
        P("dp", None),
        P("dp", None),
        P("dp", None),
        P(None, "dp", None),
        P(),
        P(),
        P(None, None, "tensor"),
        P(None, None, "tensor"),
        P(None, None, "tensor"),
        P(None, "tensor", None),
        P(),
        P(None, "dp", None, "tensor"),
        P(None, "dp", None, "tensor"),
        P(None, "dp", "tensor", None),
    )
    out_specs = (
        P("dp", None),
        P("dp", None),
        P(None, "dp"),
        P(None, "dp"),
        P(None, "dp", "tensor"),
        P(None, "dp", "tensor"),
        P(None, "dp", "tensor"),
        P(None, "tensor", "dp"),
        P(None, "dp", None),
        P(None, "dp", None, "tensor"),
        P(None, "dp", None, "tensor"),
        P(None, "dp", "tensor", None),
    )
    return jax.shard_map(
        per_device, mesh=mesh, in_specs=in_specs, out_specs=out_specs, check_vma=False
    )
```

time: 2280 us -> 486 us (0.21)
  waiting for transfers between devices: 1880 us -> 187 us
  blocking collectives: 96.5 us -> 36.6 us
  local copies, waits for them, and re-layouts: 98 us -> 39.3 us
  starting transfers between devices: 43.4 us -> 87.7 us
  matrix products: 77 us -> 43.4 us
  Pallas kernels: 0 us -> 27 us
    unnamed x23 -> x0, waiting for transfers between devices: 759 us -> none
    reduce_scatter x7 -> x0, waiting for transfers between devices: 651 us -> none  [the longest x4 168 us: from_owners(): lax.psum_scatter(partial_value.astype(jnp.bfloat16), 'tensor', scatter_di...]
    psum x4 -> x0, waiting for transfers between devices: 149 us -> none  [head_total(): return lax.psum(partial_value, 'tensor')]
    all_gather x4 -> x0, waiting for transfers between devices: 146 us -> none  [from_owners(): full = lax.all_gather(summed, 'tensor', axis=1, tiled=True)]
    ppermute x0 -> x40, waiting for transfers between devices: none -> 134 us  [swap(): return lax.ppermute(value, 'tensor', [(i, i ^ mask) for i in range(WAYS)])]
    all_to_all x6 -> x8, waiting for transfers between devices: 174 us -> 53.3 us  [exchange(): return lax.all_to_all(rows, 'dp', split_axis=0, concat_axis=0, tiled=True)]
    all_to_all x2 -> x1, blocking collectives: 96.5 us -> 36.6 us  [exchange(): return lax.all_to_all(rows, 'dp', split_axis=0, concat_axis=0, tiled=True)]
    gather x8 -> x0, local copies, waits for them, and re-layouts: 47.9 us -> none  [the longest x2 13.7 us: per_device(): picked = returned[slot]]
  transfers between devices with their start and end apart: 25 -> 48, of which waited for: 25 -> 19; matrix products, arithmetic and copies ran while one was open for 5% -> 20% of each run, Pallas kernels for 0% -> 0%
where the time goes in v1:
time: 486 us; the launch traced here: 476 us
  waiting for transfers between devices  187 us (38%)
  starting transfers between devices  87.7 us (18%)
  other arithmetic  52.3 us (11%)
  matrix products  43.4 us (9%)
  local copies, waits for them, and re-layouts  39.3 us (8%)
  blocking collectives  36.6 us (8%)
  Pallas kernels  27 us (6%)
    ppermute x40, waiting for transfers between devices, swap(): return lax.ppermute(value, 'tensor', [(i, i ^ mask) for i in range(WAYS)])  134 us
    all_to_all x8, waiting for transfers between devices, exchange(): return lax.all_to_all(rows, 'dp', split_axis=0, concat_axis=0, tiled=True)  53.3 us
    all_to_all x8, starting transfers between devices, exchange(): return lax.all_to_all(rows, 'dp', split_axis=0, concat_axis=0, tiled=True)  51.1 us
    all_to_all x1, blocking collectives, exchange(): return lax.all_to_all(rows, 'dp', split_axis=0, concat_axis=0, tiled=True)  36.6 us
    ppermute x40, starting transfers between devices, swap(): return lax.ppermute(value, 'tensor', [(i, i ^ mask) for i in range(WAYS)])  36.6 us
    dot_general x42, matrix products, dot(): lax.dot_general(a, b, (((ca,), (cb,)), ((), ())), preferred_element_type=...  29.7 us
    pallas_call x3, Pallas kernels, experts(): pl.pallas_call(functools.partial(expert_kernel, want_out, want_back), out...  27 us
  transfers between devices with their start and end apart: 48, of which 19 were waited for; matrix products, arithmetic and copies ran while one was open for 20% of the time, Pallas kernels for 0%

profile of v1, /device:TPU:0, one launch (start us, length us, event | category | flops | bytes accessed | tf_op | source)
XLA Modules:
  0.0 476.4 jit_solution(5305676834551207063)
XLA Ops:
  12.0 3.1 collective-permute-start.3
  17.3 16.3 %collective-permute-done.1 = bf16[128,1024]{1,0:T(8,128)(2,1)S(1)} collective-permute-done((bf16[128,1024]{1,0:T(8,128)(2,1)S(1)}, bf16[128,1024]{1,0:T(8,128)(2,1)S(1)}, u32[]{:S(2)}, u32[]{:S(2)}) %collective-permute-start.1) | collective-permute-done | bytes 262176 | tf_op jit(solution)/shard_map/ppermute | solution.py:110
  35.4 9.4 %all-to-all-start = ((bf16[32,16,1024]{2,1,0:T(8,128)(2,1)}), bf16[32,16,1024]{2,1,0:T(8,128)(2,1)S(1)}, u32[]{:S(2)}, u32[]{:S(2)}) async-start(bf16[32,16,1024]{2,1,0:T(8,128)(2,1)} %bitcast.28), calls=%async_computation | async-start | bytes 2097152 | tf_op jit(solution)/shard_map/all_to_all | solution.py:120
  45.6 2.7 collective-permute-start.6
  48.9 15.6 %collective-permute-done.6.refs_7_.refs_8_ = bf16[128,1024]{1,0:T(8,128)(2,1)S(1)} collective-permute-done((bf16[128,1024]{1,0:T(8,128)(2,1)S(1)}, bf16[128,1024]{1,0:T(8,128)(2,1)S(1)}, u32[]{:S(2)}, u32[]{:S(2)}) %collective-permute-start.6) | collective-permute-done | bytes 262176 | tf_op jit(solution)/shard_map/ppermute | solution.py:110
  67.9 6.0 %experts.1 = bf16[512,1024]{1,0:T(8,128)(2,1)} custom-call(bf16[512,1024]{1,0:T(8,128)(2,1)} %bitcast.315, bf16[1024,256]{1,0:T(8,128)(2,1)} %pad_maximum_fusion.3.refs_1_.refs_2_, bf16[1024,256]{1,0:T(8,128)(2,1)} %copy-done.128, bf16[1024,256]{1,0:T(8,128)(2,1)} %collective-permute-done.3.refs_3_.refs_4_, bf16[1024,256]{1,0:T(8,128)(2,1)} %copy-done.129, ...), custom_call_target="tpu_custom_call" | custom-call | flops 1610612736 | bytes 8388608 | tf_op jit(solution)/shard_map/experts/pallas_call | solution.py:177
  73.9 7.7 %all-to-all-start.1 = ((bf16[32,16,1024]{2,1,0:T(8,128)(2,1)}), bf16[32,16,1024]{2,1,0:T(8,128)(2,1)S(1)}, u32[]{:S(2)}, u32[]{:S(2)}) async-start(bf16[32,16,1024]{2,1,0:T(8,128)(2,1)} %bitcast.318), calls=%async_computation.1 | async-start | bytes 2097152 | tf_op jit(solution)/shard_map/all_to_all | solution.py:120
  82.5 17.2 %all-to-all-done.1 = bf16[32,16,1024]{2,1,0:T(8,128)(2,1)S(1)} async-done(((bf16[32,16,1024]{2,1,0:T(8,128)(2,1)}), bf16[32,16,1024]{2,1,0:T(8,128)(2,1)S(1)}, u32[]{:S(2)}, u32[]{:S(2)}) %all-to-all-start.1) | async-done | bytes 1048608 | tf_op jit(solution)/shard_map/all_to_all | solution.py:120
  101.8 2.6 collective-permute-start.9
  106.4 1.8 copy.94
  108.2 4.0 collective-permute-done.9
  117.9 2.1 collective-permute-start.11
  120.7 1.8 convolution_compare_fusion
  122.5 5.4 %collective-permute-done.11 = bf16[128,1024]{1,0:T(8,128)(2,1)} collective-permute-done((bf16[128,1024]{1,0:T(8,128)(2,1)S(1)}, bf16[128,1024]{1,0:T(8,128)(2,1)}, u32[]{:S(2)}, u32[]{:S(2)}) %collective-permute-start.11) | collective-permute-done | bytes 262176 | tf_op jit(solution)/shard_map/ppermute | solution.py:110
  132.9 1.6 pad_maximum_fusion
  134.5 4.8 %all-to-all-start.2 = ((bf16[32,32,1024]{2,1,0:T(8,128)(2,1)}), bf16[32,32,1024]{2,1,0:T(8,128)(2,1)}, u32[]{:S(2)}, u32[]{:S(2)}) async-start(bf16[32,32,1024]{2,1,0:T(8,128)(2,1)} %pad_maximum_fusion), calls=%async_computation.2 | async-start | bytes 4194304 | tf_op jit(solution)/shard_map/all_to_all | solution.py:120
  139.2 1.9 pad_maximum_fusion.4.refs_2_
  141.1 2.0 collective-permute-start.13
  144.7 32.6 %collective-permute-done.13.refs_4_ = bf16[1024,256]{1,0:T(8,128)(2,1)} collective-permute-done((bf16[1024,256]{1,0:T(8,128)(2,1)}, bf16[1024,256]{1,0:T(8,128)(2,1)}, u32[]{:S(2)}, u32[]{:S(2)}) %collective-permute-start.13) | collective-permute-done | bytes 524320 | tf_op jit(solution)/shard_map/ppermute | solution.py:110
  177.7 3.7 collective-permute-done.16.refs_8_
  181.6 3.2 fusion.183
  184.8 11.7 %experts_back.2 = (bf16[512,1024]{1,0:T(8,128)(2,1)}, bf16[512,1024]{1,0:T(8,128)(2,1)}, f32[1024,256]{1,0:T(8,128)}, bf16[1024,256]{1,0:T(8,128)(2,1)}, f32[102...) custom-call(bf16[512,1024]{1,0:T(8,128)(2,1)} %bitcast.324, ...), custom_call_target="tpu_custom_call" | custom-call | flops 4831838208 | bytes 8388608 | tf_op jit(solution)/shard_map/experts_back/pallas_call | solution.py:177
  196.5 1.8 pad_maximum_fusion.1
  198.3 36.6 %all_to_all.76 = bf16[32,32,1024]{2,1,0:T(8,128)(2,1)S(1)} all-to-all(bf16[32,32,1024]{2,1,0:T(8,128)(2,1)S(1)} %pad_maximum_fusion.1), channel_id=1, replica_groups=mesh['dp'=32,'tensor'=4] {'dp'}, dimensions={0} | all-to-all | bytes 4194304 | tf_op jit(solution)/shard_map/all_to_all | solution.py:120
  240.1 1.6 subtract_convert_fusion.1
  242.4 1.8 concatenate.103
  244.3 1.6 convolution_convert_fusion.8
  247.5 2.8 collective-permute-start.21
  252.6 6.4 %collective-permute-done.21 = bf16[128,1152]{1,0:T(8,128)(2,1)S(1)} collective-permute-done((bf16[128,1152]{1,0:T(8,128)(2,1)S(1)}, bf16[128,1152]{1,0:T(8,128)(2,1)S(1)}, u32[]{:S(2)}, u32[]{:S(2)}) %collective-permute-start.21) | collective-permute-done | bytes 294944 | tf_op jit(solution)/shard_map/ppermute | solution.py:110
  260.1 3.6 collective-permute-done.19
  266.5 1.6 copy.102
  268.1 1.8 convolution_bitcast_fusion.2
  269.9 2.2 fusion.26
  272.1 2.2 convolution_bitcast_fusion.6
  281.1 1.7 add_convert_fusion.4
  282.9 2.7 collective-permute-start.39
  286.6 1.9 add_convert_fusion
  288.5 2.7 collective-permute-start.33
  291.2 8.1 %collective-permute-done.23 = bf16[128,1024]{1,0:T(8,128)(2,1)S(1)} collective-permute-done((bf16[128,1024]{1,0:T(8,128)(2,1)S(1)}, bf16[128,1024]{1,0:T(8,128)(2,1)S(1)}, u32[]{:S(2)}, u32[]{:S(2)}) %collective-permute-start.23) | collective-permute-done | bytes 262176 | tf_op jit(solution)/shard_map/ppermute | solution.py:110
  302.6 4.7 all-to-all-start.4
  308.7 2.0 add_bitcast_fusion.2
  310.6 2.3 add_bitcast_fusion
  314.1 10.6 %all-to-all-done.4 = bf16[32,16,1024]{2,1,0:T(8,128)(2,1)} async-done(((bf16[32,16,1024]{2,1,0:T(8,128)(2,1)}), bf16[32,16,1024]{2,1,0:T(8,128)(2,1)}, u32[]{:S(2)}, u32[]{:S(2)}) %all-to-all-start.4) | async-done | bytes 1048608 | tf_op jit(solution)/shard_map/all_to_all | solution.py:120
  324.7 9.3 %experts_back.3 = (bf16[512,1024]{1,0:T(8,128)(2,1)}, f32[1024,256]{1,0:T(8,128)}, bf16[1024,256]{1,0:T(8,128)(2,1)}, f32[1024,256]{1,0:T(8,128)}, bf16[1024,256...) custom-call(bf16[512,1024]{1,0:T(8,128)(2,1)} %bitcast.316, ...), custom_call_target="tpu_custom_call" | custom-call | flops 4831838208 | bytes 8388608 | tf_op jit(solution)/shard_map/experts_back/pallas_call | solution.py:177
  334.0 5.1 %all-to-all-start.5 = ((bf16[32,16,1024]{2,1,0:T(8,128)(2,1)}), bf16[32,16,1024]{2,1,0:T(8,128)(2,1)}, u32[]{:S(2)}, u32[]{:S(2)}) async-start(bf16[32,16,1024]{2,1,0:T(8,128)(2,1)} %bitcast.317), calls=%async_computation.5 | async-start | bytes 2097152 | tf_op jit(solution)/shard_map/all_to_all | solution.py:120
  339.1 1.7 convolution_convert_fusion.16
  340.8 1.7 copy.140
  342.5 1.8 convert_element_type.643
  344.2 2.3 convolution_convert_fusion
  350.8 4.4 concatenate.120
  355.9 8.4 %all-to-all-start.8 = ((bf16[32,32,896]{2,1,0:T(8,128)(2,1)}), bf16[32,32,896]{2,1,0:T(8,128)(2,1)}, u32[]{:S(2)}, u32[]{:S(2)}) async-start(bf16[32,32,896]{2,1,0:T(8,128)(2,1)} %concatenate.120), calls=%async_computation.8 | async-start | bytes 3670016 | tf_op jit(solution)/shard_map/all_to_all | solution.py:120
  367.2 2.8 collective-permute-start.36
  370.0 2.3 add_convert_fusion.1
  373.2 2.8 collective-permute-start.25
  376.0 18.8 %collective-permute-done.36 = bf16[128,1024]{1,0:T(8,128)(2,1)S(1)} collective-permute-done((bf16[128,1024]{1,0:T(8,128)(2,1)S(1)}, bf16[128,1024]{1,0:T(8,128)(2,1)S(1)}, u32[]{:S(2)}, u32[]{:S(2)}) %collective-permute-start.36) | collective-permute-done | bytes 262176 | tf_op jit(solution)/shard_map/ppermute | solution.py:110
  397.0 14.7 %collective-permute-done.25 = bf16[128,1152]{1,0:T(8,128)(2,1)S(1)} collective-permute-done((bf16[128,1152]{1,0:T(8,128)(2,1)S(1)}, bf16[128,1152]{1,0:T(8,128)(2,1)S(1)}, u32[]{:S(2)}, u32[]{:S(2)}) %collective-permute-start.25) | collective-permute-done | bytes 294944 | tf_op jit(solution)/shard_map/ppermute | solution.py:110
  414.5 1.9 fusion.27
  416.4 2.2 convolution_bitcast_fusion.4
  426.6 7.1 %all-to-all-start.7 = ((bf16[32,32,384]{2,1,0:T(8,128)(2,1)}), bf16[32,32,384]{2,1,0:T(8,128)(2,1)}, u32[]{:S(2)}, u32[]{:S(2)}) async-start(bf16[32,32,384]{2,1,0:T(8,128)(2,1)} %maximum_maximum_fusion.1), calls=%async_computation.7 | async-start | bytes 1572864 | tf_op jit(solution)/shard_map/all_to_all | solution.py:120
  433.8 1.8 convert_reduce_fusion
  438.1 11.1 %all-to-all-done.7 = bf16[32,32,384]{2,1,0:T(8,128)(2,1)} async-done(((bf16[32,32,384]{2,1,0:T(8,128)(2,1)}), bf16[32,32,384]{2,1,0:T(8,128)(2,1)}, u32[]{:S(2)}, u32[]{:S(2)}) %all-to-all-start.7) | async-done | bytes 786464 | tf_op jit(solution)/shard_map/all_to_all | solution.py:120
  449.2 4.0 all-to-all-start.6
  453.2 1.7 add_bitcast_fusion.1
  458.8 14.3 %all-to-all-done.6 = bf16[32,32,640]{2,1,0:T(8,128)(2,1)S(1)} async-done(((bf16[32,32,640]{2,1,0:T(8,128)(2,1)}), bf16[32,32,640]{2,1,0:T(8,128)(2,1)S(1)}, u32[]{:S(2)}, u32[]{:S(2)}) %all-to-all-start.6) | async-done | bytes 1310752 | tf_op jit(solution)/shard_map/all_to_all | solution.py:120
  (485 shorter events, 95.2 us)
Async XLA Ops:
  10.1 6.3 %collective-permute-start = (bf16[128,1024]{1,0:T(8,128)(2,1)S(1)}, bf16[128,1024]{1,0:T(8,128)(2,1)S(1)}, u32[]{:S(2)}, u32[]{:S(2)}) collective-permute-start(bf16[128,1024]{1,0:T(8,128)(2,1)S(1)} %convolution_convert_fusion.11), channel_id=1, source_target_pairs={{0,1},{1,0},{2,3},{3,2},{4,5},{5,4},{6,7},{7,6},{8,9},{9,8},{10,11... | collective-permute-start | bytes 786440 | tf_op jit(solution)/shard_map/ppermute | solution.py:110
  12.0 36.4 %collective-permute-start.3 = (bf16[1024,256]{1,0:T(8,128)(2,1)}, bf16[1024,256]{1,0:T(8,128)(2,1)}, u32[]{:S(2)}, u32[]{:S(2)}) collective-permute-start(bf16[1024,256]{1,0:T(8,128)(2,1)} %pad_maximum_fusion.3.refs_1_.refs_2_), channel_id=1, source_target_pairs={{0,2},{1,3},{2,0},{3,1},{4,6},{5,7},{6,4},{7,5},{8,10},{9,11},{10,... | collective-permute-start | bytes 1572872 | tf_op jit(solution)/shard_map/ppermute | solution.py:110
  16.3 19.1 %copy-start.83 = (f32[1,1024]{1,0:T(1,128)}, f32[1,1024]{1,0:T(1,128)S(1)}, u32[]{:S(2)}) copy-start(f32[1,1024]{1,0:T(1,128)S(1)} %get-tuple-element.143) | copy-start | bytes 12292
  16.4 17.2 %collective-permute-start.1 = (bf16[128,1024]{1,0:T(8,128)(2,1)S(1)}, bf16[128,1024]{1,0:T(8,128)(2,1)S(1)}, u32[]{:S(2)}, u32[]{:S(2)}) collective-permute-start(bf16[128,1024]{1,0:T(8,128)(2,1)S(1)} %add_convert_fusion.11), channel_id=1, source_target_pairs={{0,2},{1,3},{2,0},{3,1},{4,6},{5,7},{6,4},{7,5},{8,10},{9,11},{10,... | collective-permute-start | bytes 786440 | tf_op jit(solution)/shard_map/ppermute | solution.py:110
  16.9 18.5 %copy-start.92 = (s32[512]{0:T(512)}, s32[512]{0:T(512)S(1)}, u32[]{:S(2)}) copy-start(s32[512]{0:T(512)S(1)} %get-tuple-element.167) | copy-start | bytes 6148
  17.3 18.1 %copy-start.73 = (pred[128,512]{1,0:T(32,128)(4,1)}, pred[128,512]{1,0:T(32,128)(4,1)S(1)}, u32[]{:S(2)}) copy-start(pred[128,512]{1,0:T(32,128)(4,1)S(1)} %convolution_compare_fusion.1) | copy-start | bytes 196612
  33.9 47.8 %copy-start.18 = (bf16[128,1024]{1,0:T(8,128)(2,1)}, bf16[128,1024]{1,0:T(8,128)(2,1)S(1)}, u32[]{:S(2)}) copy-start(bf16[128,1024]{1,0:T(8,128)(2,1)S(1)} %multiply_convert_fusion.2) | copy-start | bytes 786436
  35.4 31.4 %all-to-all-start = ((bf16[32,16,1024]{2,1,0:T(8,128)(2,1)}), bf16[32,16,1024]{2,1,0:T(8,128)(2,1)S(1)}, u32[]{:S(2)}, u32[]{:S(2)}) async-start(bf16[32,16,1024]{2,1,0:T(8,128)(2,1)} %bitcast.28), calls=%async_computation | async-start | bytes 2097152 | tf_op jit(solution)/shard_map/all_to_all | solution.py:120
  44.8 19.7 %collective-permute-start.2 = (bf16[1024,256]{1,0:T(8,128)(2,1)}, bf16[1024,256]{1,0:T(8,128)(2,1)S(1)}, u32[]{:S(2)}, u32[]{:S(2)}) collective-permute-start(bf16[1024,256]{1,0:T(8,128)(2,1)} %pad_maximum_fusion.3.refs_1_.refs_2_), channel_id=1, source_target_pairs={{0,1},{1,0},{2,3},{3,2},{4,5},{5,4},{6,7},{7,6},{8,9},{9,8},{10,11... | collective-permute-start | bytes 1572872 | tf_op jit(solution)/shard_map/ppermute | solution.py:110
  45.6 20.4 %copy-start.68 = (bf16[128,1024]{1,0:T(8,128)(2,1)}, bf16[128,1024]{1,0:T(8,128)(2,1)S(1)}, u32[]{:S(2)}) copy-start(bf16[128,1024]{1,0:T(8,128)(2,1)S(1)} %get-tuple-element.113.refs_5_.refs_6_) | copy-start | bytes 786436
  45.6 18.9 %collective-permute-start.6 = (bf16[128,1024]{1,0:T(8,128)(2,1)S(1)}, bf16[128,1024]{1,0:T(8,128)(2,1)S(1)}, u32[]{:S(2)}, u32[]{:S(2)}) collective-permute-start(bf16[128,1024]{1,0:T(8,128)(2,1)S(1)} %get-tuple-element.113.refs_5_.refs_6_), channel_id=1, source_target_pairs={{0,2},{1,3},{2,0},{3,1},{4,6},{5,7},{6,4},{7,5},{8,10},{9,11},{10,... | collective-permute-start | bytes 786440 | tf_op jit(solution)/shard_map/ppermute | solution.py:110
  48.4 18.4 %collective-permute-start.4 = (bf16[1024,256]{1,0:T(8,128)(2,1)}, bf16[1024,256]{1,0:T(8,128)(2,1)S(1)}, u32[]{:S(2)}, u32[]{:S(2)}) collective-permute-start(bf16[1024,256]{1,0:T(8,128)(2,1)} %collective-permute-done.3.refs_3_.refs_4_), channel_id=1, source_target_pairs={{0,1},{1,0},{2,3},{3,2},{4,5},{5,4},{6,7},{7,6},{8,9},{9,8},{10,11... | collective-permute-start | bytes 1572872 | tf_op jit(solution)/shard_map/ppermute | solution.py:110
  48.6 15.9 %collective-permute-start.5 = (bf16[128,1024]{1,0:T(8,128)(2,1)S(1)}, bf16[128,1024]{1,0:T(8,128)(2,1)S(1)}, u32[]{:S(2)}, u32[]{:S(2)}) collective-permute-start(bf16[128,1024]{1,0:T(8,128)(2,1)S(1)} %get-tuple-element.113.refs_5_.refs_6_), channel_id=1, source_target_pairs={{0,1},{1,0},{2,3},{3,2},{4,5},{5,4},{6,7},{7,6},{8,9},{9,8},{10,11... | collective-permute-start | bytes 786440 | tf_op jit(solution)/shard_map/ppermute | solution.py:110
  64.5 1.5 collective-permute-start.7
  73.9 25.9 %all-to-all-start.1 = ((bf16[32,16,1024]{2,1,0:T(8,128)(2,1)}), bf16[32,16,1024]{2,1,0:T(8,128)(2,1)S(1)}, u32[]{:S(2)}, u32[]{:S(2)}) async-start(bf16[32,16,1024]{2,1,0:T(8,128)(2,1)} %bitcast.318), calls=%async_computation.1 | async-start | bytes 2097152 | tf_op jit(solution)/shard_map/all_to_all | solution.py:120
  81.7 18.0 %copy-start.66 = (pred[128,32]{1,0:T(32,128)(4,1)}, pred[128,32]{1,0:T(32,128)(4,1)S(1)}, u32[]{:S(2)}) copy-start(pred[128,32]{1,0:T(32,128)(4,1)S(1)} %copy.92) | copy-start | bytes 12292
  82.0 17.7 %copy-start.43 = (f32[128,32]{1,0:T(8,128)}, f32[128,32]{1,0:T(8,128)S(1)}, u32[]{:S(2)}) copy-start(f32[128,32]{1,0:T(8,128)S(1)} %get-tuple-element.154) | copy-start | bytes 49156
  82.0 17.7 %copy-start.114 = (f32[128]{0:T(128)}, f32[128]{0:T(128)S(1)}, u32[]{:S(2)}) copy-start(f32[128]{0:T(128)S(1)} %get-tuple-element.153) | copy-start | bytes 1540
  82.3 17.5 %copy-start.126 = (f32[128]{0:T(128)}, f32[128]{0:T(128)S(1)}, u32[]{:S(2)}) copy-start(f32[128]{0:T(128)S(1)} %fusion.123) | copy-start | bytes 1540
  100.1 1.6 collective-permute-start.8
  101.8 10.5 %collective-permute-start.9 = (bf16[128,1024]{1,0:T(8,128)(2,1)S(1)}, bf16[128,1024]{1,0:T(8,128)(2,1)}, u32[]{:S(2)}, u32[]{:S(2)}) collective-permute-start(bf16[128,1024]{1,0:T(8,128)(2,1)S(1)} %add_convert_fusion.10), channel_id=1, source_target_pairs={{0,2},{1,3},{2,0},{3,1},{4,6},{5,7},{6,4},{7,5},{8,10},{9,11},{10,... | collective-permute-start | bytes 786440 | tf_op jit(solution)/shard_map/ppermute | solution.py:110
  116.2 1.6 collective-permute-start.10
  117.9 10.0 %collective-permute-start.11 = (bf16[128,1024]{1,0:T(8,128)(2,1)S(1)}, bf16[128,1024]{1,0:T(8,128)(2,1)}, u32[]{:S(2)}, u32[]{:S(2)}) collective-permute-start(bf16[128,1024]{1,0:T(8,128)(2,1)S(1)} %add_convert_fusion.9), channel_id=1, source_target_pairs={{0,2},{1,3},{2,0},{3,1},{4,6},{5,7},{6,4},{7,5},{8,10},{9,11},{10,... | collective-permute-start | bytes 786440 | tf_op jit(solution)/shard_map/ppermute | solution.py:110
  134.5 47.1 %all-to-all-start.2 = ((bf16[32,32,1024]{2,1,0:T(8,128)(2,1)}), bf16[32,32,1024]{2,1,0:T(8,128)(2,1)}, u32[]{:S(2)}, u32[]{:S(2)}) async-start(bf16[32,32,1024]{2,1,0:T(8,128)(2,1)} %pad_maximum_fusion), calls=%async_computation.2 | async-start | bytes 4194304 | tf_op jit(solution)/shard_map/all_to_all | solution.py:120
  141.1 36.1 %collective-permute-start.13 = (bf16[1024,256]{1,0:T(8,128)(2,1)}, bf16[1024,256]{1,0:T(8,128)(2,1)}, u32[]{:S(2)}, u32[]{:S(2)}) collective-permute-start(bf16[1024,256]{1,0:T(8,128)(2,1)} %pad_maximum_fusion.4.refs_2_), channel_id=1, source_target_pairs={{0,2},{1,3},{2,0},{3,1},{4,6},{5,7},{6,4},{7,5},{8,10},{9,11},{10,... | collective-permute-start | bytes 1572872 | tf_op jit(solution)/shard_map/ppermute | solution.py:110
  143.1 38.3 %collective-permute-start.16 = (bf16[128,1024]{1,0:T(8,128)(2,1)}, bf16[128,1024]{1,0:T(8,128)(2,1)}, u32[]{:S(2)}, u32[]{:S(2)}) collective-permute-start(bf16[128,1024]{1,0:T(8,128)(2,1)} %get-tuple-element.112.refs_6_), channel_id=1, source_target_pairs={{0,2},{1,3},{2,0},{3,1},{4,6},{5,7},{6,4},{7,5},{8,10},{9,11},{10,... | collective-permute-start | bytes 786440 | tf_op jit(solution)/shard_map/ppermute | solution.py:110
  144.6 40.1 %collective-permute-start.12 = (bf16[1024,256]{1,0:T(8,128)(2,1)}, bf16[1024,256]{1,0:T(8,128)(2,1)}, u32[]{:S(2)}, u32[]{:S(2)}) collective-permute-start(bf16[1024,256]{1,0:T(8,128)(2,1)} %pad_maximum_fusion.4.refs_2_), channel_id=1, source_target_pairs={{0,1},{1,0},{2,3},{3,2},{4,5},{5,4},{6,7},{7,6},{8,9},{9,8},{10,11... | collective-permute-start | bytes 1572872 | tf_op jit(solution)/shard_map/ppermute | solution.py:110
  177.2 7.6 %collective-permute-start.14 = (bf16[1024,256]{1,0:T(8,128)(2,1)}, bf16[1024,256]{1,0:T(8,128)(2,1)}, u32[]{:S(2)}, u32[]{:S(2)}) collective-permute-start(bf16[1024,256]{1,0:T(8,128)(2,1)} %collective-permute-done.13.refs_4_), channel_id=1, source_target_pairs={{0,1},{1,0},{2,3},{3,2},{4,5},{5,4},{6,7},{7,6},{8,9},{9,8},{10,11... | collective-permute-start | bytes 1572872 | tf_op jit(solution)/shard_map/ppermute | solution.py:110
  177.2 7.6 %collective-permute-start.15 = (bf16[128,1024]{1,0:T(8,128)(2,1)}, bf16[128,1024]{1,0:T(8,128)(2,1)}, u32[]{:S(2)}, u32[]{:S(2)}) collective-permute-start(bf16[128,1024]{1,0:T(8,128)(2,1)} %get-tuple-element.112.refs_6_), channel_id=1, source_target_pairs={{0,1},{1,0},{2,3},{3,2},{4,5},{5,4},{6,7},{7,6},{8,9},{9,8},{10,11... | collective-permute-start | bytes 786440 | tf_op jit(solution)/shard_map/ppermute | solution.py:110
  181.4 3.4 collective-permute-start.17
  244.2 2.3 collective-permute-start.20
  245.9 17.8 %copy-start.10 = (f32[128,1024]{1,0:T(8,128)S(1)}, f32[128,1024]{1,0:T(8,128)}, u32[]{:S(2)}) copy-start(f32[128,1024]{1,0:T(8,128)} %param.15) | copy-start | bytes 1572868
  245.9 5.6 %collective-permute-start.18 = (bf16[128,1024]{1,0:T(8,128)(2,1)S(1)}, bf16[128,1024]{1,0:T(8,128)(2,1)S(1)}, u32[]{:S(2)}, u32[]{:S(2)}) collective-permute-start(bf16[128,1024]{1,0:T(8,128)(2,1)S(1)} %convolution_convert_fusion.8), channel_id=1, source_target_pairs={{0,1},{1,0},{2,3},{3,2},{4,5},{5,4},{6,7},{7,6},{8,9},{9,8},{10,11... | collective-permute-start | bytes 786440 | tf_op jit(solution)/shard_map/ppermute | solution.py:110
  247.5 11.5 %collective-permute-start.21 = (bf16[128,1152]{1,0:T(8,128)(2,1)S(1)}, bf16[128,1152]{1,0:T(8,128)(2,1)S(1)}, u32[]{:S(2)}, u32[]{:S(2)}) collective-permute-start(bf16[128,1152]{1,0:T(8,128)(2,1)S(1)} %add_convert_fusion.3), channel_id=1, source_target_pairs={{0,2},{1,3},{2,0},{3,1},{4,6},{5,7},{6,4},{7,5},{8,10},{9,11},{10,... | collective-permute-start | bytes 884744 | tf_op jit(solution)/shard_map/ppermute | solution.py:110
  250.9 35.6 %collective-permute-start.32 = (bf16[1024,256]{1,0:T(8,128)(2,1)}, bf16[1024,256]{1,0:T(8,128)(2,1)}, u32[]{:S(2)}, u32[]{:S(2)}) collective-permute-start(bf16[1024,256]{1,0:T(8,128)(2,1)} %get-tuple-element.41), channel_id=1, source_target_pairs={{0,1},{1,0},{2,3},{3,2},{4,5},{5,4},{6,7},{7,6},{8,9},{9,8},{10,11... | collective-permute-start | bytes 1572872 | tf_op jit(solution)/shard_map/ppermute | solution.py:110
  250.9 30.2 %collective-permute-start.38 = (bf16[128,1024]{1,0:T(8,128)(2,1)}, bf16[128,1024]{1,0:T(8,128)(2,1)}, u32[]{:S(2)}, u32[]{:S(2)}) collective-permute-start(bf16[128,1024]{1,0:T(8,128)(2,1)} %get-tuple-element.49), channel_id=1, source_target_pairs={{0,1},{1,0},{2,3},{3,2},{4,5},{5,4},{6,7},{7,6},{8,9},{9,8},{10,11... | collective-permute-start | bytes 786440 | tf_op jit(solution)/shard_map/ppermute | solution.py:110
  251.5 12.2 %collective-permute-start.19 = (bf16[128,1024]{1,0:T(8,128)(2,1)S(1)}, bf16[128,1024]{1,0:T(8,128)(2,1)S(1)}, u32[]{:S(2)}, u32[]{:S(2)}) collective-permute-start(bf16[128,1024]{1,0:T(8,128)(2,1)S(1)} %add_convert_fusion.8), channel_id=1, source_target_pairs={{0,2},{1,3},{2,0},{3,1},{4,6},{5,7},{6,4},{7,5},{8,10},{9,11},{10,... | collective-permute-start | bytes 786440 | tf_op jit(solution)/shard_map/ppermute | solution.py:110
  279.2 20.2 %copy-start.85 = (f32[1,1024]{1,0:T(1,128)S(1)}, f32[1,1024]{1,0:T(1,128)}, u32[]{:S(2)}) copy-start(f32[1,1024]{1,0:T(1,128)} %get-tuple-element.146) | copy-start | bytes 12292
  279.2 20.2 %copy-start.121 = (f32[128]{0:T(128)S(1)}, f32[128]{0:T(128)}, u32[]{:S(2)}) copy-start(f32[128]{0:T(128)} %copy-done.120) | copy-start | bytes 1540
  279.2 6.4 %collective-permute-start.22 = (bf16[128,1024]{1,0:T(8,128)(2,1)S(1)}, bf16[128,1024]{1,0:T(8,128)(2,1)S(1)}, u32[]{:S(2)}, u32[]{:S(2)}) collective-permute-start(bf16[128,1024]{1,0:T(8,128)(2,1)S(1)} %fusion.2), channel_id=1, source_target_pairs={{0,1},{1,0},{2,3},{3,2},{4,5},{5,4},{6,7},{7,6},{8,9},{9,8},{10,11... | collective-permute-start | bytes 786440 | tf_op jit(solution)/shard_map/ppermute | solution.py:110
  280.6 30.0 %collective-permute-start.31 = (bf16[1024,256]{1,0:T(8,128)(2,1)}, bf16[1024,256]{1,0:T(8,128)(2,1)}, u32[]{:S(2)}, u32[]{:S(2)}) collective-permute-start(bf16[1024,256]{1,0:T(8,128)(2,1)} %get-tuple-element.39), channel_id=1, source_target_pairs={{0,1},{1,0},{2,3},{3,2},{4,5},{5,4},{6,7},{7,6},{8,9},{9,8},{10,11... | collective-permute-start | bytes 1572872 | tf_op jit(solution)/shard_map/ppermute | solution.py:110
  281.1 27.5 %collective-permute-start.37 = (bf16[128,1024]{1,0:T(8,128)(2,1)}, bf16[128,1024]{1,0:T(8,128)(2,1)}, u32[]{:S(2)}, u32[]{:S(2)}) collective-permute-start(bf16[128,1024]{1,0:T(8,128)(2,1)} %get-tuple-element.47), channel_id=1, source_target_pairs={{0,1},{1,0},{2,3},{3,2},{4,5},{5,4},{6,7},{7,6},{8,9},{9,8},{10,11... | collective-permute-start | bytes 786440 | tf_op jit(solution)/shard_map/ppermute | solution.py:110
  282.9 17.3 %copy-start.3 = (f32[128,1024]{1,0:T(8,128)S(1)}, f32[128,1024]{1,0:T(8,128)}, u32[]{:S(2)}) copy-start(f32[128,1024]{1,0:T(8,128)} %copy-done.2) | copy-start | bytes 1572868
  282.9 25.8 %collective-permute-start.39 = (bf16[128,1024]{1,0:T(8,128)(2,1)}, bf16[128,1024]{1,0:T(8,128)(2,1)}, u32[]{:S(2)}, u32[]{:S(2)}) collective-permute-start(bf16[128,1024]{1,0:T(8,128)(2,1)} %add_convert_fusion.4), channel_id=1, source_target_pairs={{0,2},{1,3},{2,0},{3,1},{4,6},{5,7},{6,4},{7,5},{8,10},{9,11},{10,... | collective-permute-start | bytes 786440 | tf_op jit(solution)/shard_map/ppermute | solution.py:110
  285.7 13.7 %collective-permute-start.23 = (bf16[128,1024]{1,0:T(8,128)(2,1)S(1)}, bf16[128,1024]{1,0:T(8,128)(2,1)S(1)}, u32[]{:S(2)}, u32[]{:S(2)}) collective-permute-start(bf16[128,1024]{1,0:T(8,128)(2,1)S(1)} %add_convert_fusion.7), channel_id=1, source_target_pairs={{0,2},{1,3},{2,0},{3,1},{4,6},{5,7},{6,4},{7,5},{8,10},{9,11},{10,... | collective-permute-start | bytes 786440 | tf_op jit(solution)/shard_map/ppermute | solution.py:110
  288.5 22.1 %collective-permute-start.33 = (bf16[1024,256]{1,0:T(8,128)(2,1)}, bf16[1024,256]{1,0:T(8,128)(2,1)}, u32[]{:S(2)}, u32[]{:S(2)}) collective-permute-start(bf16[1024,256]{1,0:T(8,128)(2,1)} %add_convert_fusion), channel_id=1, source_target_pairs={{0,2},{1,3},{2,0},{3,1},{4,6},{5,7},{6,4},{7,5},{8,10},{9,11},{10,... | collective-permute-start | bytes 1572872 | tf_op jit(solution)/shard_map/ppermute | solution.py:110
  302.6 22.1 %all-to-all-start.4 = ((bf16[32,16,1024]{2,1,0:T(8,128)(2,1)}), bf16[32,16,1024]{2,1,0:T(8,128)(2,1)}, u32[]{:S(2)}, u32[]{:S(2)}) async-start(bf16[32,16,1024]{2,1,0:T(8,128)(2,1)} %bitcast.305), calls=%async_computation.4 | async-start | bytes 2097152 | tf_op jit(solution)/shard_map/all_to_all | solution.py:120
  334.0 21.9 %all-to-all-start.5 = ((bf16[32,16,1024]{2,1,0:T(8,128)(2,1)}), bf16[32,16,1024]{2,1,0:T(8,128)(2,1)}, u32[]{:S(2)}, u32[]{:S(2)}) async-start(bf16[32,16,1024]{2,1,0:T(8,128)(2,1)} %bitcast.317), calls=%async_computation.5 | async-start | bytes 2097152 | tf_op jit(solution)/shard_map/all_to_all | solution.py:120
  348.1 21.9 %collective-permute-start.29 = (bf16[1024,256]{1,0:T(8,128)(2,1)}, bf16[1024,256]{1,0:T(8,128)(2,1)}, u32[]{:S(2)}, u32[]{:S(2)}) collective-permute-start(bf16[1024,256]{1,0:T(8,128)(2,1)} %get-tuple-element.37), channel_id=1, source_target_pairs={{0,1},{1,0},{2,3},{3,2},{4,5},{5,4},{6,7},{7,6},{8,9},{9,8},{10,11... | collective-permute-start | bytes 1572872 | tf_op jit(solution)/shard_map/ppermute | solution.py:110
  348.2 17.9 %collective-permute-start.35 = (bf16[128,1024]{1,0:T(8,128)(2,1)}, bf16[128,1024]{1,0:T(8,128)(2,1)}, u32[]{:S(2)}, u32[]{:S(2)}) collective-permute-start(bf16[128,1024]{1,0:T(8,128)(2,1)} %get-tuple-element.45), channel_id=1, source_target_pairs={{0,1},{1,0},{2,3},{3,2},{4,5},{5,4},{6,7},{7,6},{8,9},{9,8},{10,11... | collective-permute-start | bytes 786440 | tf_op jit(solution)/shard_map/ppermute | solution.py:110
  355.3 97.9 %collective-permute-start.28 = (bf16[1024,256]{1,0:T(8,128)(2,1)}, bf16[1024,256]{1,0:T(8,128)(2,1)}, u32[]{:S(2)}, u32[]{:S(2)}) collective-permute-start(bf16[1024,256]{1,0:T(8,128)(2,1)} %get-tuple-element.35), channel_id=1, source_target_pairs={{0,1},{1,0},{2,3},{3,2},{4,5},{5,4},{6,7},{7,6},{8,9},{9,8},{10,11... | collective-permute-start | bytes 1572872 | tf_op jit(solution)/shard_map/ppermute | solution.py:110
  355.4 20.6 %collective-permute-start.34 = (bf16[128,1024]{1,0:T(8,128)(2,1)}, bf16[128,1024]{1,0:T(8,128)(2,1)}, u32[]{:S(2)}, u32[]{:S(2)}) collective-permute-start(bf16[128,1024]{1,0:T(8,128)(2,1)} %get-tuple-element.43), channel_id=1, source_target_pairs={{0,1},{1,0},{2,3},{3,2},{4,5},{5,4},{6,7},{7,6},{8,9},{9,8},{10,11... | collective-permute-start | bytes 786440 | tf_op jit(solution)/shard_map/ppermute | solution.py:110
  355.9 70.7 %all-to-all-start.8 = ((bf16[32,32,896]{2,1,0:T(8,128)(2,1)}), bf16[32,32,896]{2,1,0:T(8,128)(2,1)}, u32[]{:S(2)}, u32[]{:S(2)}) async-start(bf16[32,32,896]{2,1,0:T(8,128)(2,1)} %concatenate.120), calls=%async_computation.8 | async-start | bytes 3670016 | tf_op jit(solution)/shard_map/all_to_all | solution.py:120
  366.0 28.9 %copy-start.46 = (f32[128,1024]{1,0:T(8,128)S(1)}, f32[128,1024]{1,0:T(8,128)}, u32[]{:S(2)}) copy-start(f32[128,1024]{1,0:T(8,128)} %get-tuple-element.42) | copy-start | bytes 1572868
  366.0 7.1 %collective-permute-start.24 = (bf16[128,1152]{1,0:T(8,128)(2,1)S(1)}, bf16[128,1152]{1,0:T(8,128)(2,1)S(1)}, u32[]{:S(2)}, u32[]{:S(2)}) collective-permute-start(bf16[128,1152]{1,0:T(8,128)(2,1)S(1)} %concatenate.106), channel_id=1, source_target_pairs={{0,1},{1,0},{2,3},{3,2},{4,5},{5,4},{6,7},{7,6},{8,9},{9,8},{10,11... | collective-permute-start | bytes 884744 | tf_op jit(solution)/shard_map/ppermute | solution.py:110
  367.2 27.7 %collective-permute-start.36 = (bf16[128,1024]{1,0:T(8,128)(2,1)S(1)}, bf16[128,1024]{1,0:T(8,128)(2,1)S(1)}, u32[]{:S(2)}, u32[]{:S(2)}) collective-permute-start(bf16[128,1024]{1,0:T(8,128)(2,1)S(1)} %add_convert_fusion.5), channel_id=1, source_target_pairs={{0,2},{1,3},{2,0},{3,1},{4,6},{5,7},{6,4},{7,5},{8,10},{9,11},{10,... | collective-permute-start | bytes 786440 | tf_op jit(solution)/shard_map/ppermute | solution.py:110
  370.0 26.0 %copy-start.23 = (f32[1,128,1024]{2,1,0:T(8,128)S(1)}, f32[1,128,1024]{2,1,0:T(8,128)}, u32[]{:S(2)}) copy-start(f32[1,128,1024]{2,1,0:T(8,128)} %add_bitcast_fusion.2) | copy-start | bytes 1572868
  372.3 80.9 %collective-permute-start.30 = (bf16[1024,256]{1,0:T(8,128)(2,1)}, bf16[1024,256]{1,0:T(8,128)(2,1)}, u32[]{:S(2)}, u32[]{:S(2)}) collective-permute-start(bf16[1024,256]{1,0:T(8,128)(2,1)} %add_convert_fusion.1), channel_id=1, source_target_pairs={{0,2},{1,3},{2,0},{3,1},{4,6},{5,7},{6,4},{7,5},{8,10},{9,11},{10,... | collective-permute-start | bytes 1572872 | tf_op jit(solution)/shard_map/ppermute | solution.py:110
  373.2 38.5 %collective-permute-start.25 = (bf16[128,1152]{1,0:T(8,128)(2,1)S(1)}, bf16[128,1152]{1,0:T(8,128)(2,1)S(1)}, u32[]{:S(2)}, u32[]{:S(2)}) collective-permute-start(bf16[128,1152]{1,0:T(8,128)(2,1)S(1)} %add_convert_fusion.2), channel_id=1, source_target_pairs={{0,2},{1,3},{2,0},{3,1},{4,6},{5,7},{6,4},{7,5},{8,10},{9,11},{10,... | collective-permute-start | bytes 884744 | tf_op jit(solution)/shard_map/ppermute | solution.py:110
  394.8 16.9 %copy-start.123 = (f32[128]{0:T(128)S(1)}, f32[128]{0:T(128)}, u32[]{:S(2)}) copy-start(f32[128]{0:T(128)} %copy-done.122) | copy-start | bytes 1540
  422.4 3.3 collective-permute-start.26
  425.7 10.3 %collective-permute-start.27 = (bf16[128,1024]{1,0:T(8,128)(2,1)S(1)}, bf16[128,1024]{1,0:T(8,128)(2,1)S(1)}, u32[]{:S(2)}, u32[]{:S(2)}) collective-permute-start(bf16[128,1024]{1,0:T(8,128)(2,1)S(1)} %add_convert_fusion.6), channel_id=1, source_target_pairs={{0,2},{1,3},{2,0},{3,1},{4,6},{5,7},{6,4},{7,5},{8,10},{9,11},{10,... | collective-permute-start | bytes 786440 | tf_op jit(solution)/shard_map/ppermute | solution.py:110
  426.6 22.5 %all-to-all-start.7 = ((bf16[32,32,384]{2,1,0:T(8,128)(2,1)}), bf16[32,32,384]{2,1,0:T(8,128)(2,1)}, u32[]{:S(2)}, u32[]{:S(2)}) async-start(bf16[32,32,384]{2,1,0:T(8,128)(2,1)} %maximum_maximum_fusion.1), calls=%async_computation.7 | async-start | bytes 1572864 | tf_op jit(solution)/shard_map/all_to_all | solution.py:120
  449.2 23.9 %all-to-all-start.6 = ((bf16[32,32,640]{2,1,0:T(8,128)(2,1)}), bf16[32,32,640]{2,1,0:T(8,128)(2,1)S(1)}, u32[]{:S(2)}, u32[]{:S(2)}) async-start(bf16[32,32,640]{2,1,0:T(8,128)(2,1)} %maximum_maximum_fusion), calls=%async_computation.6 | async-start | bytes 2621440 | tf_op jit(solution)/shard_map/all_to_all | solution.py:120
  (118 other events, 589.4 us)
